TPU v7x, 32 devices: a whole 2x2x4 slice. The times are simulated.
32 devices in a mesh: frame: 8 (over z, y), row: 4 (over x, core).
Axes of the slice: x: 2, y: 2, z: 4, core: 2. Of those that a mesh axis runs over, the one named last changes fastest.
Arguments:
- frames_x: bfloat16 [8, 24, 128, 512], P('frame', 'row'), may hold values from -6 to 6
- conv_weight: bfloat16 [3, 3, 512, 512], replicated, may hold values from -0.09375 to 0.09375
- conv_bias: float32 [512], replicated, may hold values from -3 to 3
- query_weight: bfloat16 [512, 512], replicated, may hold values from -0.25 to 0.25
- key_weight: bfloat16 [512, 512], replicated, may hold values from -0.25 to 0.25
- value_weight: bfloat16 [512, 512], replicated, may hold values from -0.25 to 0.25
- out_weight: bfloat16 [512, 512], replicated, may hold values from -0.25 to 0.25
- query_gain: float32 [512], replicated, may hold values from 0.5 to 2
- key_gain: float32 [512], replicated, may hold values from 0.5 to 2
- source_ids: int32 [8, 24, 4], P('frame', 'row'), may hold values from 0 to 23, as said below
- valid_counts: int32 [8, 24], P('frame', 'row'), may hold values from 1 to 4
Outputs:
- propagated: bfloat16 [8, 24, 128, 512], P('frame', 'row')
Inputs may be any that keep to these rules, and one draw needn't show every extreme that they name: `source_ids`: block id s names row s // 1 of the previous frame, which lies at most 2 rows from the querying block's row; in every frame slot 0 of the blocks in even rows names a block 2 rows above and in odd rows 2 rows below, as far as the frame has that row.
All inputs are finite; a program needn't handle non-finite values.
Results may differ from a plain program's by a relative error of at most 0.0054.
Values may be sent and summed in bfloat16 or wider, within the bound.
A program may use at most 64 MiB of HBM per device.

v0:
```python
import jax
import jax.numpy as jnp
from jax import lax
from jax.sharding import PartitionSpec as P

HEADS = 8
HD = 64
KSRC = 4
BLOCK = 128
DISP = 2


def with_halo(shard, sides, width):
    for axis, dim in sides:
        peers, length = (lax.axis_size(axis), shard.shape[dim])
        up = [(i, (i + 1) % peers) for i in range(peers - 1)]
        down = [(j, i) for i, j in up]
        last = lax.slice_in_dim(shard, length - width, length, axis=dim)
        initial = lax.slice_in_dim(shard, 0, width, axis=dim)
        before = lax.ppermute(last, axis, up)
        after = lax.ppermute(initial, axis, down)
        shard = jnp.concatenate([before, shard, after], axis=dim)
    return shard


def shifted(block, axis, distance):
    devices = range(lax.axis_size(axis))
    route = [(i - distance, i) for i in devices if i - distance in devices]
    return lax.ppermute(block, axis, route)


def normed(feats, weight, gain):
    proj = jnp.dot(feats, weight, preferred_element_type=jnp.float32).reshape(-1, HEADS, HD)
    proj = (
        proj
        * lax.rsqrt(jnp.mean(proj * proj, axis=-1, keepdims=True) + 1e-06)
        * gain.reshape(HEADS, HD)
    )
    return proj.reshape(-1, HEADS * HD).astype(jnp.bfloat16)


def shards(
    frames_x,
    conv_weight,
    conv_bias,
    query_weight,
    key_weight,
    value_weight,
    out_weight,
    query_gain,
    key_gain,
    source_ids,
    valid_counts,
):
    band_rows = frames_x.shape[1]
    width = frames_x.shape[2]
    chans = frames_x.shape[3]
    per_row = width // BLOCK
    tokens = band_rows * width
    nblocks = band_rows * per_row
    extended = with_halo(frames_x, (("row", 1),), 1)[0]
    padded = jnp.pad(extended, ((0, 0), (1, 1), (0, 0)))
    total = jnp.zeros((tokens, chans), jnp.float32)
    for row_off in range(3):
        for col_off in range(3):
            window = padded[row_off : row_off + band_rows, col_off : col_off + width].reshape(
                tokens, chans
            )
            total = total + jnp.dot(
                window, conv_weight[row_off, col_off], preferred_element_type=jnp.float32
            )
    feats = (total + conv_bias).astype(jnp.bfloat16)
    queries = normed(feats, query_weight, query_gain)
    keys_own = normed(feats, key_weight, key_gain)
    values_own = jnp.dot(feats, value_weight, preferred_element_type=jnp.float32).astype(
        jnp.bfloat16
    )
    reach_rows = band_rows + 2 * DISP
    earlier = shifted(feats.reshape(1, band_rows, width, chans), "frame", 1)
    reached = with_halo(earlier, (("row", 1),), DISP)[0]
    reached = reached.reshape(reach_rows * width, chans)
    prev_keys = normed(reached, key_weight, key_gain)
    prev_values = jnp.dot(reached, value_weight, preferred_element_type=jnp.float32).astype(
        jnp.bfloat16
    )
    prev_pairs = jnp.concatenate([prev_keys, prev_values], axis=-1).reshape(
        reach_rows * per_row, BLOCK, 2 * chans
    )
    frame_pos = lax.axis_index("frame")
    band_pos = lax.axis_index("row")
    local_ids = source_ids[0] - (band_pos * band_rows - DISP) * per_row
    picked = jnp.take(prev_pairs, local_ids, axis=0)
    key_set = jnp.concatenate(
        [keys_own.reshape(nblocks, 1, BLOCK, chans), picked[..., :chans]], axis=1
    )
    value_set = jnp.concatenate(
        [values_own.reshape(nblocks, 1, BLOCK, chans), picked[..., chans:]], axis=1
    )
    key_heads = key_set.reshape(nblocks, -1, HEADS, HD)
    value_heads = value_set.reshape(nblocks, -1, HEADS, HD)
    query_heads = queries.reshape(nblocks, BLOCK, HEADS, HD)
    slots = (jnp.arange(KSRC, dtype=jnp.int32)[None, :] < valid_counts[0][:, None]) & (
        frame_pos > 0
    )
    slot_mask = jnp.concatenate([jnp.ones((nblocks, 1), dtype=bool), slots], axis=1)
    mask = jnp.repeat(slot_mask, BLOCK, axis=1)
    scores = jnp.einsum(
        "nqhd,nkhd->nhqk", query_heads, key_heads, preferred_element_type=jnp.float32
    ) * HD ** (-0.5)
    expo = jnp.where(mask[:, None, None, :], jnp.exp(scores), 0.0)
    probs = (expo / jnp.sum(expo, axis=-1, keepdims=True)).astype(jnp.bfloat16)
    mixed = jnp.einsum("nhqk,nkhd->nqhd", probs, value_heads, preferred_element_type=jnp.float32)
    mixed = mixed.reshape(tokens, chans).astype(jnp.bfloat16)
    result = feats.astype(jnp.float32) + jnp.dot(
        mixed, out_weight, preferred_element_type=jnp.float32
    )
    return result.astype(jnp.bfloat16).reshape(1, band_rows, width, chans)


def solution(mesh):
    return jax.shard_map(
        shards,
        mesh=mesh,
        in_specs=(
            P("frame", "row", None, None),
            P(),
            P(),
            P(),
            P(),
            P(),
            P(),
            P(),
            P(),
            P("frame", "row", None),
            P("frame", "row"),
        ),
        out_specs=P("frame", "row", None, None),
        check_vma=False,
    )
```

profile of v0, /device:TPU:26, one launch (start us, length us, event | category | flops | bytes accessed | tf_op | source)
XLA Modules:
  0.0 138.6 jit_solution(6146243044968278645)
XLA Ops:
  0.0 1.8 %fusion.41 = (bf16[1,1,128,512]{3,2,1,0:T(8,128)(2,1)}, bf16[1,1,128,512]{3,2,1,0:T(8,128)(2,1)}) fusion(bf16[1,6,128,512]{3,2,1,0:T(8,128)(2,1)} %param.11), kind=kLoop, calls=%fused_computation.79 | loop fusion | bytes 524288 | tf_op jit(solution)/shard_map/slice | solution.py:18
  1.8 1.9 %collective-permute-start = (bf16[1,1,128,512]{3,2,1,0:T(8,128)(2,1)}, bf16[1,1,128,512]{3,2,1,0:T(8,128)(2,1)S(1)}, u32[]{:S(2)}, u32[]{:S(2)}) collective-permute-start(bf16[1,1,128,512]{3,2,1,0:T(8,128)(2,1)} %get-tuple-element.17), channel_id=1, source_target_pairs={{0,1},{1,2},{2,3},{4,5},{5,6},{6,7},{8,9},{9,10},{10,11},{12,13},{... | collective-permute-start | bytes 393224 | tf_op jit(solution)/shard_map/ppermute | solution.py:20
  3.8 3.6 %collective-permute-start.1 = (bf16[1,1,128,512]{3,2,1,0:T(8,128)(2,1)}, bf16[1,1,128,512]{3,2,1,0:T(8,128)(2,1)}, u32[]{:S(2)}, u32[]{:S(2)}) collective-permute-start(bf16[1,1,128,512]{3,2,1,0:T(8,128)(2,1)} %get-tuple-element.18), channel_id=1, source_target_pairs={{1,0},{2,1},{3,2},{5,4},{6,5},{7,6},{9,8},{10,9},{11,10},{13,12},{... | collective-permute-start | bytes 393224 | tf_op jit(solution)/shard_map/ppermute | solution.py:21
  7.4 0.7 fusion.36
  8.1 0.7 broadcast_bitcast_fusion
  8.8 0.7 compare_select_fusion
  9.5 1.8 %fusion.17 = f32[768,512]{1,0:T(8,128)S(1)} fusion(bf16[768,512]{1,0:T(8,128)(2,1)} %bitcast.112, bf16[3,3,512,512]{3,2,1,0:T(8,128)(2,1)} %param.12), kind=kOutput, calls=%fused_computation.43 | convolution fusion | flops 402653184 | bytes 2883584 | tf_op jit(solution)/shard_map/dot_general | solution.py:69
  11.3 0.7 copy.20
  12.3 1.0 copy.21
  13.3 1.2 pad_maximum_fusion.3
  14.5 1.7 %fusion.23 = f32[768,512]{1,0:T(8,128)S(1)} fusion(bf16[768,512]{1,0:T(8,128)(2,1)S(1)} %bitcast.119, bf16[3,3,512,512]{3,2,1,0:T(8,128)(2,1)} %param.12), kind=kOutput, calls=%fused_computation.49 | convolution fusion | flops 402653184 | bytes 2883584 | tf_op jit(solution)/shard_map/dot_general | solution.py:69
  16.3 1.1 maximum_bitcast_fusion
  17.4 0.6 pad_slice_fusion.5
  19.2 0.6 fusion.19
  20.9 0.6 fusion.10
  21.5 1.2 add_convert_fusion.1
  22.7 1.8 %fusion.42 = (f32[768,512]{1,0:T(8,128)}, f32[768,512]{1,0:T(8,128)S(1)}) fusion(bf16[768,512]{1,0:T(8,128)(2,1)S(1)} %add_convert_fusion.1, bf16[512,512]{1,0:T(8,128)(2,1)S(1)} %copy-done.11), kind=kOutput, calls=%fused_computation.80 | convolution fusion | flops 403046400 | bytes 4456448 | tf_op jit(solution)/shard_map/dot_general | solution.py:33
  24.4 3.4 %collective-permute-start.2 = (bf16[1,6,128,512]{3,2,1,0:T(8,128)(2,1)S(1)}, bf16[1,6,128,512]{3,2,1,0:T(8,128)(2,1)}, u32[]{:S(2)}, u32[]{:S(2)}) collective-permute-start(bf16[1,6,128,512]{3,2,1,0:T(8,128)(2,1)S(1)} %bitcast.113), channel_id=1, source_target_pairs={{0,4},{4,8},{8,12},{12,16},{16,20},{20,24},{24,28},{1,5},{5,9},{9,... | collective-permute-start | bytes 2359304 | tf_op jit(solution)/shard_map/ppermute | solution.py:29
  27.9 3.0 %copy.26 = f32[768,512]{0,1:T(8,128)} copy(f32[768,512]{1,0:T(8,128)} %get-tuple-element.21) | data formatting | bytes 3145728 | tf_op jit(solution)/shard_map/mul | solution.py:36
  30.9 1.5 %bitcast_reduce_fusion = f32[768,8]{0,1:T(8,128)S(1)} fusion(f32[768,512]{0,1:T(8,128)} %copy.26), kind=kLoop, calls=%fused_computation.12 | loop fusion | flops 387072 | bytes 1597440 | tf_op jit(solution)/shard_map/reduce_sum | solution.py:36
  32.5 1.3 mul.98
  33.8 3.0 %copy.27 = f32[768,512]{1,0:T(8,128)} copy(f32[768,512]{0,1:T(8,128)} %bitcast.114) | data formatting | bytes 3145728 | tf_op jit(solution)/shard_map/mul | solution.py:35
  36.8 1.8 %bitcast_reduce_fusion.1 = (f32[768,8]{0,1:T(8,128)S(1)}, f32[768,512]{0,1:T(8,128)}) fusion(bf16[768,512]{1,0:T(8,128)(2,1)S(1)} %add_convert_fusion.1, bf16[512,512]{1,0:T(8,128)(2,1)S(1)} %copy-done.14), kind=kOutput, calls=%fused_computation.16 | convolution fusion | flops 403433472 | bytes 2908160 | tf_op jit(solution)/shard_map/dot_general | solution.py:33
  38.6 1.3 multiply_convert_fusion.1
  39.9 6.3 %collective-permute-done.2 = bf16[1,6,128,512]{3,2,1,0:T(8,128)(2,1)} collective-permute-done((bf16[1,6,128,512]{3,2,1,0:T(8,128)(2,1)S(1)}, bf16[1,6,128,512]{3,2,1,0:T(8,128)(2,1)}, u32[]{:S(2)}, u32[]{:S(2)}) %collective-permute-start.2) | collective-permute-done | bytes 786464 | tf_op jit(solution)/shard_map/ppermute | solution.py:29
  46.2 1.9 %fusion.40 = (bf16[1,2,128,512]{3,2,1,0:T(8,128)(2,1)}, bf16[1,2,128,512]{3,2,1,0:T(8,128)(2,1)}) fusion(bf16[1,6,128,512]{3,2,1,0:T(8,128)(2,1)} %collective-permute-done.2), kind=kLoop, calls=%fused_computation.78 | loop fusion | bytes 1048576 | tf_op jit(solution)/shard_map/slice | solution.py:19
  48.1 1.9 %collective-permute-start.3 = (bf16[1,2,128,512]{3,2,1,0:T(8,128)(2,1)}, bf16[1,2,128,512]{3,2,1,0:T(8,128)(2,1)S(1)}, u32[]{:S(2)}, u32[]{:S(2)}) collective-permute-start(bf16[1,2,128,512]{3,2,1,0:T(8,128)(2,1)} %get-tuple-element.14), channel_id=1, source_target_pairs={{0,1},{1,2},{2,3},{4,5},{5,6},{6,7},{8,9},{9,10},{10,11},{12,13},{... | collective-permute-start | bytes 786440 | tf_op jit(solution)/shard_map/ppermute | solution.py:20
  50.0 1.5 %convolution_convert_fusion.1 = bf16[768,512]{1,0:T(8,128)(2,1)} fusion(bf16[768,512]{1,0:T(8,128)(2,1)S(1)} %add_convert_fusion.1, bf16[512,512]{1,0:T(8,128)(2,1)S(1)} %copy-done), kind=kOutput, calls=%fused_computation.20 | convolution fusion | flops 403046400 | bytes 2097152 | tf_op jit(solution)/shard_map/dot_general | solution.py:75
  51.5 3.8 %collective-permute-start.4 = (bf16[1,2,128,512]{3,2,1,0:T(8,128)(2,1)}, bf16[1,2,128,512]{3,2,1,0:T(8,128)(2,1)S(1)}, u32[]{:S(2)}, u32[]{:S(2)}) collective-permute-start(bf16[1,2,128,512]{3,2,1,0:T(8,128)(2,1)} %get-tuple-element.13), channel_id=1, source_target_pairs={{1,0},{2,1},{3,2},{5,4},{6,5},{7,6},{9,8},{10,9},{11,10},{13,12},{... | collective-permute-start | bytes 786440 | tf_op jit(solution)/shard_map/ppermute | solution.py:21
  55.3 4.8 %copy.25 = bf16[6,1,128,512]{2,1,3,0:T(2,128)(2,1)} copy(bf16[6,1,128,512]{3,2,0,1:T(8,128)(2,1)} %bitcast.128) | data formatting | bytes 1572864 | tf_op jit(solution)/shard_map/reshape | solution.py:97
  60.1 1.1 fusion.3
  61.2 2.7 %reshape.147 = bf16[6,128,8,64]{1,0,3,2:T(8,128)(2,1)} reshape(bf16[768,512]{0,1:T(8,128)(2,1)} %fusion.3) | data formatting | bytes 1572864 | tf_op jit(solution)/shard_map/reshape | solution.py:101
  63.9 2.9 %copy.28 = bf16[6,1,128,512]{2,1,3,0:T(2,128)(2,1)} copy(bf16[6,1,128,512]{3,2,0,1:T(8,128)(2,1)S(1)} %bitcast.118) | data formatting | bytes 1572864 | tf_op jit(solution)/shard_map/reshape | solution.py:94
  66.8 1.2 constant_dynamic-update-slice_fusion.1
  68.1 0.9 convolution_convert_fusion
  69.0 0.9 multiply_reduce_fusion
  70.3 1.7 %pad_maximum_fusion.2 = bf16[1280,1024]{0,1:T(8,128)(2,1)} fusion(bf16[1280,512]{0,1:T(8,128)(2,1)S(1)} %convolution_convert_fusion, bf16[1280,512]{0,1:T(8,128)(2,1)S(1)} %bitcast.115), kind=kLoop, calls=%fused_computation.9 | loop fusion | flops 5242880 | bytes 5242880 | tf_op jit(solution)/shard_map/concatenate | solution.py:86
  72.0 3.0 %copy.22 = bf16[1280,1024]{1,0:T(8,128)(2,1)S(1)} copy(bf16[1280,1024]{0,1:T(8,128)(2,1)} %pad_maximum_fusion.2) | data formatting | bytes 5242880 | tf_op jit(solution)/shard_map/concatenate | solution.py:86
  75.0 4.4 %gather_fusion = bf16[24,128,1024]{2,1,0:T(8,128)(2,1)} fusion(bf16[10,128,1024]{2,1,0:T(8,128)(2,1)S(1)} %bitcast.110, s32[1024]{0:T(1024)S(1)} %pad_clamp_fusion), kind=kCustom, calls=%fused_computation | custom fusion | bytes 12583008 | tf_op jit(solution)/shard_map/jit(_take)/gather | solution.py:92
  79.4 10.6 %copy.24 = bf16[6,4,128,1024]{2,1,3,0:T(4,128)(2,1)} copy(bf16[6,4,128,1024]{3,2,1,0:T(8,128)(2,1)} %bitcast.111) | data formatting | bytes 12582912 | tf_op jit(solution)/shard_map/jit(_take)/gather | solution.py:92
  89.9 5.6 %broadcast_select_fusion = bf16[6,4,128,1024]{2,1,3,0:T(4,128)(2,1)S(1)} fusion(bf16[6,4,128,1024]{2,1,3,0:T(4,128)(2,1)} %copy.24, pred[6,4]{1,0:T(8,128)(4,1)S(1)} %copy-done.20), kind=kLoop, calls=%fused_computation.7 | loop fusion | flops 3145728 | bytes 12582936 | tf_op jit(solution)/shard_map/jit(_take)/select_n | solution.py:92
  95.5 2.2 %fusion.39 = (bf16[6,4,128,512]{2,1,3,0:T(4,128)(2,1)S(1)}, bf16[6,4,128,512]{2,1,3,0:T(4,128)(2,1)S(1)}) fusion(bf16[6,4,128,1024]{2,1,3,0:T(4,128)(2,1)S(1)} %broadcast_select_fusion), kind=kLoop, calls=%fused_computation.77 | loop fusion | bytes 12582912 | tf_op jit(solution)/shard_map/slice | solution.py:94
  97.8 8.6 %pad_maximum_fusion = (bf16[6,5,128,512]{2,1,3,0:T(8,128)(2,1)}, bf16[6,5,128,512]{2,1,3,0:T(8,128)(2,1)}) fusion(bf16[6,4,128,512]{2,1,3,0:T(4,128)(2,1)S(1)} %get-tuple-element.6, bf16[6,1,128,512]{2,1,3,0:T(2,128)(2,1)S(1)} %copy-done.7, bf16[6,4,128,512]{2,1,3,0:T(4,128)(2,1)S(1)} %get-tuple-element.5, bf16[6,1,128,512]{2,1,3,0:T(2,128)(2,1)S(1)} %copy-done.8), kind=kLoop, calls=%fused_computation.5 | loop fusion | flops 15728640 | bytes 15728640 | tf_op jit(solution)/shard_map/concatenate | solution.py:96
  106.3 9.8 %reshape.146 = bf16[6,640,8,64]{1,3,2,0:T(8,128)(2,1)} reshape(bf16[6,5,128,512]{2,1,3,0:T(8,128)(2,1)} %get-tuple-element.27) | data formatting | bytes 7864320 | tf_op jit(solution)/shard_map/reshape | solution.py:100
  116.2 10.1 %reshape.149 = bf16[6,640,8,64]{1,3,2,0:T(8,128)(2,1)} reshape(bf16[6,5,128,512]{2,1,3,0:T(8,128)(2,1)} %get-tuple-element.28) | data formatting | bytes 7864320 | tf_op jit(solution)/shard_map/reshape | solution.py:99
  126.3 5.6 %fusion = (f32[6,8,128]{2,1,0:T(8,128)S(1)}, f32[6,8,128,640]{3,2,1,0:T(8,128)S(1)}) fusion(pred[6,640]{1,0:T(8,128)(4,1)S(1)} %copy-done.17, bf16[6,640,8,64]{1,3,2,0:T(8,128)(2,1)} %reshape.149, bf16[6,128,8,64]{1,0,3,2:T(8,128)(2,1)S(1)} %copy-done.12), kind=kOutput, calls=%fused_computation.3 | convolution fusion | flops 515106816 | bytes 20475648 | tf_op jit(solution)/shard_map/nqhd,nkhd->nhqk/dot_general | solution.py:107
  131.9 4.6 %fusion.5 = bf16[6,128,8,64]{1,3,2,0:T(8,128)(2,1)S(1)} fusion(bf16[6,640,8,64]{1,3,2,0:T(8,128)(2,1)S(1)} %copy-done.9, f32[6,8,128,640]{3,2,1,0:T(8,128)S(1)} %get-tuple-element.26, f32[6,8,128]{2,1,0:T(8,128)S(1)} %get-tuple-element.25, pred[6,640]{1,0:T(8,128)(4,1)S(1)} %copy-done.17), kind=kOutput, calls=%fused_computation.22 | convolution fusion | flops 519438336 | bytes 20475648 | tf_op jit(solution)/shard_map/nhqk,nkhd->nqhd/dot_general | solution.py:112
  137.1 1.5 %add_convert_fusion = bf16[768,512]{1,0:T(8,128)(2,1)} fusion(bf16[768,512]{1,0:T(8,128)(2,1)S(1)} %copy-done.4, bf16[512,512]{1,0:T(8,128)(2,1)S(1)} %copy-done.21, bf16[64,8,6,128]{3,2,1,0:T(8,128)(2,1)S(1)} %bitcast.127), kind=kOutput, calls=%fused_computation.17 | convolution fusion | flops 403832832 | bytes 2883584 | tf_op jit(solution)/shard_map/dot_general | solution.py:114
  (70 shorter events, 3.7 us)
Async XLA Ops:
  0.0 50.0 %copy-start = (bf16[512,512]{1,0:T(8,128)(2,1)S(1)}, bf16[512,512]{1,0:T(8,128)(2,1)}, u32[]{:S(2)}) copy-start(bf16[512,512]{1,0:T(8,128)(2,1)} %param.16) | copy-start | bytes 1572868
  0.0 13.3 %copy-start.2 = (bf16[1,6,128,512]{3,2,1,0:T(8,128)(2,1)S(1)}, bf16[1,6,128,512]{3,2,1,0:T(8,128)(2,1)}, u32[]{:S(2)}) copy-start(bf16[1,6,128,512]{3,2,1,0:T(8,128)(2,1)} %param.11) | copy-start | bytes 2359300
  0.0 11.3 %copy-start.16 = (s32[1,6,4]{1,2,0:T(4,128)S(1)}, s32[1,6,4]{1,2,0:T(4,128)}, u32[]{:S(2)}) copy-start(s32[1,6,4]{1,2,0:T(4,128)} %param.20) | copy-start | bytes 292
  0.0 12.2 %copy-start.15 = (f32[512]{0:T(512)S(1)}, f32[512]{0:T(512)}, u32[]{:S(2)}) copy-start(f32[512]{0:T(512)} %param.19) | copy-start | bytes 6148
  0.0 12.2 %copy-start.11 = (bf16[512,512]{1,0:T(8,128)(2,1)S(1)}, bf16[512,512]{1,0:T(8,128)(2,1)}, u32[]{:S(2)}) copy-start(bf16[512,512]{1,0:T(8,128)(2,1)} %param.15) | copy-start | bytes 1572868
  1.8 11.4 %collective-permute-start = (bf16[1,1,128,512]{3,2,1,0:T(8,128)(2,1)}, bf16[1,1,128,512]{3,2,1,0:T(8,128)(2,1)S(1)}, u32[]{:S(2)}, u32[]{:S(2)}) collective-permute-start(bf16[1,1,128,512]{3,2,1,0:T(8,128)(2,1)} %get-tuple-element.17), channel_id=1, source_target_pairs={{0,1},{1,2},{2,3},{4,5},{5,6},{6,7},{8,9},{9,10},{10,11},{12,13},{... | collective-permute-start | bytes 393224 | tf_op jit(solution)/shard_map/ppermute | solution.py:20
  3.8 9.5 %collective-permute-start.1 = (bf16[1,1,128,512]{3,2,1,0:T(8,128)(2,1)}, bf16[1,1,128,512]{3,2,1,0:T(8,128)(2,1)}, u32[]{:S(2)}, u32[]{:S(2)}) collective-permute-start(bf16[1,1,128,512]{3,2,1,0:T(8,128)(2,1)} %get-tuple-element.18), channel_id=1, source_target_pairs={{1,0},{2,1},{3,2},{5,4},{6,5},{7,6},{9,8},{10,9},{11,10},{13,12},{... | collective-permute-start | bytes 393224 | tf_op jit(solution)/shard_map/ppermute | solution.py:21
  13.3 4.7 %slice-start = ((s8[4718592]{0:T(1024)(128)(4,1)}), s8[4194304]{0:T(1024)(128)(4,1)S(1)}, s32[]{:S(2)}) async-start(s8[4718592]{0:T(1024)(128)(4,1)} %bitcast.116), calls=%async_computation | async-start | bytes 8388608
  16.2 1.8 %slice-start.1 = ((s8[4718592]{0:T(1024)(128)(4,1)}), s8[524288]{0:T(1024)(128)(4,1)S(1)}, s32[]{:S(2)}) async-start(s8[4718592]{0:T(1024)(128)(4,1)} %bitcast.116), calls=%async_computation.1 | async-start | bytes 1048576
  20.3 1.2 copy-start.19
  22.7 27.3 %copy-start.3 = (bf16[768,512]{1,0:T(8,128)(2,1)}, bf16[768,512]{1,0:T(8,128)(2,1)S(1)}, u32[]{:S(2)}) copy-start(bf16[768,512]{1,0:T(8,128)(2,1)S(1)} %add_convert_fusion.1) | copy-start | bytes 2359300
  24.4 21.7 %collective-permute-start.2 = (bf16[1,6,128,512]{3,2,1,0:T(8,128)(2,1)S(1)}, bf16[1,6,128,512]{3,2,1,0:T(8,128)(2,1)}, u32[]{:S(2)}, u32[]{:S(2)}) collective-permute-start(bf16[1,6,128,512]{3,2,1,0:T(8,128)(2,1)S(1)} %bitcast.113), channel_id=1, source_target_pairs={{0,4},{4,8},{8,12},{12,16},{16,20},{20,24},{24,28},{1,5},{5,9},{9,... | collective-permute-start | bytes 2359304 | tf_op jit(solution)/shard_map/ppermute | solution.py:29
  32.4 4.4 %copy-start.14 = (bf16[512,512]{1,0:T(8,128)(2,1)S(1)}, bf16[512,512]{1,0:T(8,128)(2,1)}, u32[]{:S(2)}) copy-start(bf16[512,512]{1,0:T(8,128)(2,1)} %param.14) | copy-start | bytes 1572868
  36.8 1.8 %copy-start.5 = (f32[768,512]{1,0:T(8,128)S(1)}, f32[768,512]{1,0:T(8,128)}, u32[]{:S(2)}) copy-start(f32[768,512]{1,0:T(8,128)} %copy.27) | copy-start | bytes 4718596
  39.9 20.2 %copy-start.6 = (f32[768,512]{0,1:T(8,128)S(1)}, f32[768,512]{0,1:T(8,128)}, u32[]{:S(2)}) copy-start(f32[768,512]{0,1:T(8,128)} %get-tuple-element.24) | copy-start | bytes 4718596
  39.9 20.2 %copy-start.18 = (f32[512]{0:T(512)S(1)}, f32[512]{0:T(512)}, u32[]{:S(2)}) copy-start(f32[512]{0:T(512)} %param.18) | copy-start | bytes 6148
  48.1 18.7 %collective-permute-start.3 = (bf16[1,2,128,512]{3,2,1,0:T(8,128)(2,1)}, bf16[1,2,128,512]{3,2,1,0:T(8,128)(2,1)S(1)}, u32[]{:S(2)}, u32[]{:S(2)}) collective-permute-start(bf16[1,2,128,512]{3,2,1,0:T(8,128)(2,1)} %get-tuple-element.14), channel_id=1, source_target_pairs={{0,1},{1,2},{2,3},{4,5},{5,6},{6,7},{8,9},{9,10},{10,11},{12,13},{... | collective-permute-start | bytes 786440 | tf_op jit(solution)/shard_map/ppermute | solution.py:20
  51.5 16.6 %collective-permute-start.4 = (bf16[1,2,128,512]{3,2,1,0:T(8,128)(2,1)}, bf16[1,2,128,512]{3,2,1,0:T(8,128)(2,1)S(1)}, u32[]{:S(2)}, u32[]{:S(2)}) collective-permute-start(bf16[1,2,128,512]{3,2,1,0:T(8,128)(2,1)} %get-tuple-element.13), channel_id=1, source_target_pairs={{1,0},{2,1},{3,2},{5,4},{6,5},{7,6},{9,8},{10,9},{11,10},{13,12},{... | collective-permute-start | bytes 786440 | tf_op jit(solution)/shard_map/ppermute | solution.py:21
  60.1 3.8 %copy-start.10 = (bf16[768,512]{1,0:T(8,128)(2,1)S(1)}, bf16[768,512]{1,0:T(8,128)(2,1)}, u32[]{:S(2)}) copy-start(bf16[768,512]{1,0:T(8,128)(2,1)} %multiply_convert_fusion.1) | copy-start | bytes 2359300
  66.8 2.2 %copy-start.13 = (bf16[512,512]{0,1:T(8,128)(2,1)S(1)}, bf16[512,512]{0,1:T(8,128)(2,1)}, u32[]{:S(2)}) copy-start(bf16[512,512]{0,1:T(8,128)(2,1)} %copy.21) | copy-start | bytes 1572868
  79.4 10.6 %copy-start.20 = (pred[6,4]{1,0:T(8,128)(4,1)S(1)}, pred[6,4]{1,0:T(8,128)(4,1)}, u32[]{:S(2)}) copy-start(pred[6,4]{1,0:T(8,128)(4,1)} %copy.20) | copy-start | bytes 76
  95.5 2.3 %copy-start.7 = (bf16[6,1,128,512]{2,1,3,0:T(2,128)(2,1)S(1)}, bf16[6,1,128,512]{2,1,3,0:T(2,128)(2,1)}, u32[]{:S(2)}) copy-start(bf16[6,1,128,512]{2,1,3,0:T(2,128)(2,1)} %copy.25) | copy-start | bytes 2359300
  95.5 2.3 %copy-start.8 = (bf16[6,1,128,512]{2,1,3,0:T(2,128)(2,1)S(1)}, bf16[6,1,128,512]{2,1,3,0:T(2,128)(2,1)}, u32[]{:S(2)}) copy-start(bf16[6,1,128,512]{2,1,3,0:T(2,128)(2,1)} %copy.28) | copy-start | bytes 2359300
  116.2 10.1 %copy-start.12 = (bf16[6,128,8,64]{1,0,3,2:T(8,128)(2,1)S(1)}, bf16[6,128,8,64]{1,0,3,2:T(8,128)(2,1)}, u32[]{:S(2)}) copy-start(bf16[6,128,8,64]{1,0,3,2:T(8,128)(2,1)} %reshape.147) | copy-start | bytes 2359300
  116.2 10.1 %copy-start.17 = (pred[6,640]{1,0:T(8,128)(4,1)S(1)}, pred[6,640]{1,0:T(8,128)(4,1)}, u32[]{:S(2)}) copy-start(pred[6,640]{1,0:T(8,128)(4,1)} %broadcast_bitcast_fusion) | copy-start | bytes 11524
  126.3 5.6 %copy-start.9 = (bf16[6,640,8,64]{1,3,2,0:T(8,128)(2,1)S(1)}, bf16[6,640,8,64]{1,3,2,0:T(8,128)(2,1)}, u32[]{:S(2)}) copy-start(bf16[6,640,8,64]{1,3,2,0:T(8,128)(2,1)} %reshape.146) | copy-start | bytes 11796484
  131.8 5.2 %copy-start.4 = (bf16[768,512]{1,0:T(8,128)(2,1)S(1)}, bf16[768,512]{1,0:T(8,128)(2,1)}, u32[]{:S(2)}) copy-start(bf16[768,512]{1,0:T(8,128)(2,1)} %copy-done.3) | copy-start | bytes 2359300
  131.9 5.2 %copy-start.21 = (bf16[512,512]{1,0:T(8,128)(2,1)S(1)}, bf16[512,512]{1,0:T(8,128)(2,1)}, u32[]{:S(2)}) copy-start(bf16[512,512]{1,0:T(8,128)(2,1)} %param.17) | copy-start | bytes 1572868
  131.9 6.7 %copy-start.1 = (bf16[512,512]{1,0:T(8,128)(2,1)S(1)}, bf16[512,512]{1,0:T(8,128)(2,1)}, u32[]{:S(2)}) copy-start(bf16[512,512]{1,0:T(8,128)(2,1)} %param.16) | copy-start | bytes 1572868
where the time goes:
time: 140 us; the launch traced here: 139 us
  local copies, waits for them, and re-layouts  66.7 us (48%)
  matrix products  26.6 us (19%)
  other arithmetic  23.8 us (17%)
  starting transfers between devices  14.7 us (10%)
  waiting for transfers between devices  6.31 us (5%)
    gather x2, local copies, waits for them, and re-layouts, shards(): picked = jnp.take(prev_pairs, local_ids, axis=0)  15 us
    reshape x1, local copies, waits for them, and re-layouts, shards(): key_heads = key_set.reshape(nblocks, -1, HEADS, HD)  10.1 us
    reshape x1, local copies, waits for them, and re-layouts, shards(): value_heads = value_set.reshape(nblocks, -1, HEADS, HD)  9.81 us
    concatenate x1, other arithmetic, shards(): jnp.concatenate([values_own.reshape(nblocks, 1, BLOCK, chans), picked[......  8.58 us
    dot_general x9, matrix products, shards(): jnp.dot(window, conv_weight[row_off, col_off], preferred_element_type=jnp...  8.15 us
    ppermute x2, starting transfers between devices, with_halo(): after = lax.ppermute(initial, axis, down)  7.46 us
    ppermute x1, waiting for transfers between devices, shifted(): return lax.ppermute(block, axis, route)  6.3 us
    select_n x2, other arithmetic, shards(): picked = jnp.take(prev_pairs, local_ids, axis=0)  6.24 us
  transfers between devices with their start and end apart: 5, of which 1 were waited for; matrix products, arithmetic and copies ran while one was open for 23% of the time, Pallas kernels for 0%

commit v1 on v0

v1 whole, which is shorter than its diff:
```python
import functools

import jax
import jax.numpy as jnp
from jax import lax
from jax.experimental import pallas as pl
from jax.experimental.pallas import tpu as pltpu
from jax.sharding import PartitionSpec as P

HEADS = 8
HD = 64
KSRC = 4
DISP = 2
GROUP = 4
F32 = jnp.float32
BF16 = jnp.bfloat16


def dot(a, b):
    return jnp.dot(a, b, preferred_element_type=F32)


def shift_columns(left, mid, right, width):
    count = mid.shape[0]
    col = lax.broadcasted_iota(jnp.int32, mid.shape, 0) % width
    return (
        mid
        + jnp.where(col == 0, 0.0, pltpu.roll(left, 1, 0))
        + jnp.where(col == width - 1, 0.0, pltpu.roll(right, count - 1, 0))
    )


def head_mean(chans):
    row = lax.broadcasted_iota(jnp.int32, (chans, chans), 0) // HD
    col = lax.broadcasted_iota(jnp.int32, (chans, chans), 1) // HD
    return jnp.where(row == col, 1.0 / HD, 0.0).astype(BF16)


def normed(feats, weight, gain, mean, scale):
    proj = dot(feats, weight)
    square = dot((proj * proj).astype(BF16), mean)
    out = (proj * lax.rsqrt(square + 1e-06) * gain).astype(BF16)
    return out * scale if scale != 1 else out


def conv_kernel(top, mid, bottom, weight, bias, feats, ext, left, centre, right):
    tap = pl.program_id(0)
    rows, width, chans = mid.shape
    count = rows * width

    @pl.when(tap == 0)
    def _():
        ext[0:width] = top[0]
        ext[width : width + count] = mid[...].reshape(count, chans)
        ext[width + count :] = bottom[0]

    window = ext[pl.ds(pl.multiple_of(tap * width, width), count)]
    for which, acc in enumerate((left, centre, right)):
        part = dot(window, weight[0, which])

        @pl.when(tap == 0)
        def _():
            acc[...] = part

        @pl.when(tap > 0)
        def _():
            acc[...] += part

    @pl.when(tap == 2)
    def _():
        total = shift_columns(left[...], centre[...], right[...], width)
        feats[...] = (total + bias[...]).astype(BF16)


def own_kernel(feats, wq, wk, wv, gq, gk, q, k, v):
    mean = head_mean(feats.shape[1])
    f = feats[...]
    q[...] = normed(f, wq[...], gq[...], mean, HD**-0.5)
    k[...] = normed(f, wk[...], gk[...], mean, 1)
    v[...] = dot(f, wv[...]).astype(BF16)


def attend_kernel(ids, valid, feats, q, k, v, above, prev, below, wk, wv, wo, gk, out, keys, values, mixed):
    nblocks, width, chans = q.shape
    mean = head_mean(chans)
    keys[0:nblocks] = k[...]
    values[0:nblocks] = v[...]
    at = nblocks
    for part in (above, prev, below):
        rows = part.shape[0]
        f = part[...].reshape(rows * width, chans)
        keys[at : at + rows] = normed(f, wk[...], gk[...], mean, 1).reshape(rows, width, chans)
        values[at : at + rows] = dot(f, wv[...]).astype(BF16).reshape(rows, width, chans)
        at += rows
    lanes = GROUP * HD
    head = lax.broadcasted_iota(jnp.int32, (1, lanes), 1) // HD
    slot = lax.broadcasted_iota(jnp.int32, (1, (1 + KSRC) * width), 1) // width

    def block(n, carry):
        places = [n] + [nblocks + ids[n, j] for j in range(KSRC)]
        mask = slot <= valid[n]
        for g in range(chans // lanes):
            cut = pl.ds(g * lanes, lanes)
            key = jnp.concatenate([keys[p, :, cut] for p in places], axis=0)
            value = jnp.concatenate([values[p, :, cut] for p in places], axis=0)
            query = q[n, :, cut]
            stack = jnp.concatenate(
                [jnp.where(head == h, query, jnp.zeros_like(query)) for h in range(GROUP)], axis=0
            )
            scores = lax.dot_general(
                stack, key, (((1,), (1,)), ((), ())), preferred_element_type=F32
            )
            expo = jnp.where(mask, jnp.exp(scores), 0.0)
            total = jnp.sum(expo, axis=1, keepdims=True)
            part = dot(expo.astype(BF16), value) / total
            joined = part[0:width]
            for h in range(1, GROUP):
                joined = jnp.where(head == h, part[h * width : (h + 1) * width], joined)
            mixed[n, :, cut] = joined.astype(BF16)
        return carry

    lax.fori_loop(0, nblocks, block, 0)
    flat = mixed[...].reshape(nblocks * width, chans)
    f = feats[...].reshape(nblocks * width, chans).astype(F32)
    out[...] = (f + dot(flat, wo[...])).astype(BF16).reshape(nblocks, width, chans)


VM = pl.BlockSpec(memory_space=pltpu.VMEM)
SM = pl.BlockSpec(memory_space=pltpu.SMEM)
PARAMS = dict(vmem_limit_bytes=48 * 2**20)


def shape(*dims):
    return jax.ShapeDtypeStruct(dims, BF16)


def edges(block, width):
    peers = lax.axis_size("row")
    up = [(i, i + 1) for i in range(peers - 1)]
    down = [(i + 1, i) for i in range(peers - 1)]
    rows = block.shape[0]
    before = lax.ppermute(block[rows - width :], "row", up)
    after = lax.ppermute(block[:width], "row", down)
    return before, after


def shards(x, wc, bias, wq, wk, wv, wo, gq, gk, source_ids, valid_counts):
    x = x[0]
    rows, width, chans = x.shape
    count = rows * width
    gq, gk, bias = gq[None], gk[None], bias[None]
    top, bottom = edges(x, 1)
    feats = pl.pallas_call(
        conv_kernel,
        grid=(3,),
        out_shape=shape(count, chans),
        in_specs=[VM, VM, VM, pl.BlockSpec((1, 3, chans, chans), lambda a: (a, 0, 0, 0)), VM],
        out_specs=VM,
        scratch_shapes=[pltpu.VMEM((count + 2 * width, chans), BF16)]
        + [pltpu.VMEM((count, chans), F32)] * 3,
        compiler_params=pltpu.CompilerParams(**PARAMS),
    )(top, x, bottom, wc, bias)
    frames = lax.axis_size("frame")
    prev = lax.ppermute(
        feats.reshape(rows, width, chans), "frame", [(i, i + 1) for i in range(frames - 1)]
    )
    q, k, v = pl.pallas_call(
        own_kernel,
        out_shape=(shape(count, chans),) * 3,
        in_specs=[VM] * 6,
        out_specs=(VM,) * 3,
        compiler_params=pltpu.CompilerParams(**PARAMS),
        cost_estimate=pl.CostEstimate(
            flops=10 * count * chans * chans, bytes_accessed=8 * count * chans, transcendentals=0
        ),
    )(feats, wq, wk, wv, gq, gk)
    above, below = edges(prev, DISP)
    ids = source_ids[0] - (lax.axis_index("row") * rows - DISP)
    valid = jnp.where(lax.axis_index("frame") > 0, valid_counts[0], 0)
    blocked = (rows, width, chans)
    out = pl.pallas_call(
        attend_kernel,
        out_shape=shape(*blocked),
        in_specs=[SM, SM] + [VM] * 11,
        out_specs=VM,
        scratch_shapes=[pltpu.VMEM((2 * rows + 2 * DISP, width, chans), BF16)] * 2
        + [pltpu.VMEM(blocked, BF16)],
        compiler_params=pltpu.CompilerParams(**PARAMS),
    )(
        ids,
        valid,
        feats.reshape(blocked),
        q.reshape(blocked),
        k.reshape(blocked),
        v.reshape(blocked),
        above,
        prev,
        below,
        wk,
        wv,
        wo,
        gk,
    )
    return out[None]


def solution(mesh):
    return jax.shard_map(
        shards,
        mesh=mesh,
        in_specs=(P("frame", "row", None, None),)
        + (P(),) * 8
        + (P("frame", "row", None), P("frame", "row")),
        out_specs=P("frame", "row", None, None),
        check_vma=False,
    )
```

time: 140 us -> 62.5 us (0.45)
  local copies, waits for them, and re-layouts: 66.7 us -> 4.83 us
  matrix products: 26.6 us -> 0 us
  other arithmetic: 23.8 us -> 0.01 us
  Pallas kernels: 0 us -> 22.1 us
  waiting for transfers between devices: 6.31 us -> 22.8 us
  starting transfers between devices: 14.7 us -> 12.3 us
    reshape x5 -> x0, local copies, waits for them, and re-layouts: 30.3 us -> none  [the longest x1 10.1 us: shards(): key_heads = key_set.reshape(nblocks, -1, HEADS, HD)]
    dot_general x17 -> x0, matrix products: 26.6 us -> none  [the longest x9 8.15 us: shards(): jnp.dot(window, conv_weight[row_off, col_off], preferred_element_type=jnp...]
    pallas_call x0 -> x3, Pallas kernels: none -> 22.1 us  [the longest x1 11.7 us: shards(): pl.pallas_call(attend_kernel, out_shape=shape(*blocked), in_specs=[SM, SM...]
    ppermute x5, waiting for transfers between devices: 6.31 us -> 22.8 us  [the longest x1 16.2 us: shards(): lax.ppermute(feats.reshape(rows, width, chans), 'frame', [(i, i + 1) for...]
    gather x2 -> x0, local copies, waits for them, and re-layouts: 15 us -> none  [shards(): picked = jnp.take(prev_pairs, local_ids, axis=0)]
    concatenate x3 -> x0, other arithmetic: 11.5 us -> none  [the longest x1 8.58 us: shards(): jnp.concatenate([values_own.reshape(nblocks, 1, BLOCK, chans), picked[......]
    mul x4 -> x0, local copies, waits for them, and re-layouts: 7.42 us -> none  [the longest x3 4.4 us: normed(): proj * lax.rsqrt(jnp.mean(proj * proj, axis=-1, keepdims=True) + 1e-06)]
    select_n x2 -> x1, other arithmetic: 6.24 us -> 0.01 us  [shards(): valid = jnp.where(lax.axis_index('frame') > 0, valid_counts[0], 0)]
  transfers between devices with their start and end apart: 5 -> 5, of which waited for: 1 -> 4; matrix products, arithmetic and copies ran while one was open for 23% -> 0% of each run, Pallas kernels for 0% -> 4%
where the time goes in v1:
time: 62.5 us; the launch traced here: 62.1 us
  waiting for transfers between devices  22.8 us (36%)
  Pallas kernels  22.1 us (35%)
  starting transfers between devices  12.3 us (20%)
  local copies, waits for them, and re-layouts  4.83 us (8%)
    ppermute x1, waiting for transfers between devices, shards(): lax.ppermute(feats.reshape(rows, width, chans), 'frame', [(i, i + 1) for...  16.2 us
    pallas_call x1, Pallas kernels, shards(): pl.pallas_call(attend_kernel, out_shape=shape(*blocked), in_specs=[SM, SM...  11.7 us
    pallas_call x1, Pallas kernels, shards(): pl.pallas_call(conv_kernel, grid=(3,), out_shape=shape(count, chans), in_...  8.16 us
    ppermute x2, waiting for transfers between devices, edges(): before = lax.ppermute(block[rows - width:], 'row', up)  6.44 us
    ppermute x2, starting transfers between devices, edges(): after = lax.ppermute(block[:width], 'row', down)  4.38 us
    ppermute x2, starting transfers between devices, edges(): before = lax.ppermute(block[rows - width:], 'row', up)  4.33 us
    ppermute x1, starting transfers between devices, shards(): lax.ppermute(feats.reshape(rows, width, chans), 'frame', [(i, i + 1) for...  3.56 us
    unnamed x20, local copies, waits for them, and re-layouts  2.88 us
  transfers between devices with their start and end apart: 5, of which 4 were waited for; matrix products, arithmetic and copies ran while one was open for 0% of the time, Pallas kernels for 4%

profile of v1, /device:TPU:26, one launch (start us, length us, event | category | flops | bytes accessed | tf_op | source)
XLA Modules:
  0.0 62.1 jit_solution(2124853679101625954)
XLA Ops:
  0.0 0.0 copy-start.8
  0.0 0.0 copy-start.9
  0.0 0.0 copy-start.1
  0.0 0.0 copy-start.5
  0.0 0.0 copy-start.7
  0.0 1.0 %slice_bitcast_fusion = (bf16[1,128,512]{2,1,0:T(8,128)(2,1)S(1)}, bf16[1,128,512]{2,1,0:T(8,128)(2,1)S(1)}) fusion(bf16[1,6,128,512]{3,2,1,0:T(8,128)(2,1)} %param.11), kind=kLoop, calls=%fused_computation | loop fusion | bytes 524288 | tf_op jit(solution)/shard_map/slice | solution.py:143
  1.1 1.9 %collective-permute-start.1 = (bf16[1,128,512]{2,1,0:T(8,128)(2,1)S(1)}, bf16[1,128,512]{2,1,0:T(8,128)(2,1)S(1)}, u32[]{:S(2)}, u32[]{:S(2)}) collective-permute-start(bf16[1,128,512]{2,1,0:T(8,128)(2,1)S(1)} %get-tuple-element.13), channel_id=1, source_target_pairs={{1,0},{2,1},{3,2},{5,4},{6,5},{7,6},{9,8},{10,9},{11,10},{13,12},{... | collective-permute-start | bytes 393224 | tf_op jit(solution)/shard_map/ppermute | solution.py:143
  3.0 2.4 %collective-permute-start = (bf16[1,128,512]{2,1,0:T(8,128)(2,1)S(1)}, bf16[1,128,512]{2,1,0:T(8,128)(2,1)S(1)}, u32[]{:S(2)}, u32[]{:S(2)}) collective-permute-start(bf16[1,128,512]{2,1,0:T(8,128)(2,1)S(1)} %get-tuple-element.14), channel_id=1, source_target_pairs={{0,1},{1,2},{2,3},{4,5},{5,6},{6,7},{8,9},{9,10},{10,11},{12,13},{... | collective-permute-start | bytes 393224 | tf_op jit(solution)/shard_map/ppermute | solution.py:142
  5.4 0.1 collective-permute-done.1.bottom
  5.5 3.8 %collective-permute-done.top = bf16[1,128,512]{2,1,0:T(8,128)(2,1)S(1)} collective-permute-done((bf16[1,128,512]{2,1,0:T(8,128)(2,1)S(1)}, bf16[1,128,512]{2,1,0:T(8,128)(2,1)S(1)}, u32[]{:S(2)}, u32[]{:S(2)}) %collective-permute-start) | collective-permute-done | bytes 131104 | tf_op jit(solution)/shard_map/ppermute | solution.py:142
  9.3 0.0 copy-start
  9.3 1.1 %copy-done = bf16[1,6,128,512]{3,2,1,0:T(8,128)(2,1)S(1)} copy-done((bf16[1,6,128,512]{3,2,1,0:T(8,128)(2,1)S(1)}, bf16[1,6,128,512]{3,2,1,0:T(8,128)(2,1)}, u32[]{:S(2)}) %copy-start) | copy-done | bytes 786456
  10.4 0.0 copy-start.4
  10.4 0.7 %copy-done.4 = f32[512]{0:T(512)S(1)} copy-done((f32[512]{0:T(512)S(1)}, f32[512]{0:T(512)}, u32[]{:S(2)}) %copy-start.4) | copy-done | bytes 2072
  11.1 0.0 copy-start.2
  11.1 8.2 %shard_map.109.feats = bf16[768,512]{1,0:T(8,128)(2,1)S(1)} custom-call(bf16[1,128,512]{2,1,0:T(8,128)(2,1)S(1)} %collective-permute-done.top, bf16[6,128,512]{2,1,0:T(8,128)(2,1)S(1)} %bitcast.19, bf16[1,128,512]{2,1,0:T(8,128)(2,1)S(1)} %collective-permute-done.1.bottom, bf16[3,3,512,512]{3,2,1,0:T(8,128)(2,1)} %weight.1, f32[1,512]{1,0:T(1,128)S(1)} %bitcast.23), custom_call_target="tpu_custom_call" | custom-call | tf_op jit(solution)/shard_map/pallas_call | solution.py:153
  19.3 0.0 copy-start.3
  19.3 3.6 %collective-permute-start.2 = (bf16[6,128,512]{2,1,0:T(8,128)(2,1)S(1)}, bf16[6,128,512]{2,1,0:T(8,128)(2,1)S(1)}, u32[]{:S(2)}, u32[]{:S(2)}) collective-permute-start(bf16[6,128,512]{2,1,0:T(8,128)(2,1)S(1)} %bitcast.17), channel_id=1, source_target_pairs={{0,4},{4,8},{8,12},{12,16},{16,20},{20,24},{24,28},{1,5},{5,9},{9,... | collective-permute-start | bytes 2359304 | tf_op jit(solution)/shard_map/ppermute | solution.py:164
  22.9 0.0 copy-done.8
  22.9 16.2 %collective-permute-done.2.prev = bf16[6,128,512]{2,1,0:T(8,128)(2,1)S(1)} collective-permute-done((bf16[6,128,512]{2,1,0:T(8,128)(2,1)S(1)}, bf16[6,128,512]{2,1,0:T(8,128)(2,1)S(1)}, u32[]{:S(2)}, u32[]{:S(2)}) %collective-permute-start.2) | collective-permute-done | bytes 786464 | tf_op jit(solution)/shard_map/ppermute | solution.py:164
  39.1 0.8 %fusion.1 = (bf16[2,128,512]{2,1,0:T(8,128)(2,1)}, bf16[2,128,512]{2,1,0:T(8,128)(2,1)}) fusion(bf16[6,128,512]{2,1,0:T(8,128)(2,1)S(1)} %collective-permute-done.2.prev), kind=kLoop, calls=%fused_computation.5 | loop fusion | bytes 1048576 | tf_op jit(solution)/shard_map/slice | solution.py:143
  39.9 2.5 %collective-permute-start.4 = (bf16[2,128,512]{2,1,0:T(8,128)(2,1)}, bf16[2,128,512]{2,1,0:T(8,128)(2,1)S(1)}, u32[]{:S(2)}, u32[]{:S(2)}) collective-permute-start(bf16[2,128,512]{2,1,0:T(8,128)(2,1)} %get-tuple-element.11), channel_id=1, source_target_pairs={{1,0},{2,1},{3,2},{5,4},{6,5},{7,6},{9,8},{10,9},{11,10},{13,12},{... | collective-permute-start | bytes 786440 | tf_op jit(solution)/shard_map/ppermute | solution.py:143
  42.4 1.9 %collective-permute-start.3 = (bf16[2,128,512]{2,1,0:T(8,128)(2,1)}, bf16[2,128,512]{2,1,0:T(8,128)(2,1)}, u32[]{:S(2)}, u32[]{:S(2)}) collective-permute-start(bf16[2,128,512]{2,1,0:T(8,128)(2,1)} %get-tuple-element.12), channel_id=1, source_target_pairs={{0,1},{1,2},{2,3},{4,5},{5,6},{6,7},{8,9},{9,10},{10,11},{12,13},{... | collective-permute-start | bytes 786440 | tf_op jit(solution)/shard_map/ppermute | solution.py:142
  44.3 0.0 copy-done.9
  44.4 0.1 copy.12.ids
  44.4 0.0 copy-done.1
  44.4 0.0 copy-done.5
  44.5 0.0 copy-done.7
  44.5 0.0 copy-done.2
  44.5 0.0 copy-start.6
  44.5 1.0 %copy-done.6 = bf16[512,512]{1,0:T(8,128)(2,1)S(1)} copy-done((bf16[512,512]{1,0:T(8,128)(2,1)S(1)}, bf16[512,512]{1,0:T(8,128)(2,1)}, u32[]{:S(2)}) %copy-start.6) | copy-done | bytes 524312
  45.5 2.2 %shard_map.110 = (bf16[768,512]{1,0:T(8,128)(2,1)S(1)}, bf16[768,512]{1,0:T(8,128)(2,1)S(1)}, bf16[768,512]{1,0:T(8,128)(2,1)S(1)}) custom-call(bf16[768,512]{1,0:T(8,128)(2,1)S(1)} %shard_map.109.feats, bf16[512,512]{1,0:T(8,128)(2,1)S(1)} %copy-done.6, bf16[512,512]{1,0:T(8,128)(2,1)S(1)} %copy-done.1, bf16[512,512]{1,0:T(8,128)(2,1)S(1)} %copy-done.2, ...), custom_call_target="tpu_custom_call" | custom-call | flops 2013265920 | bytes 3145728 | tf_op jit(solution)/shard_map/pallas_call | solution.py:167
  47.7 0.0 collective-permute-done.4.below
  47.7 2.7 %collective-permute-done.3.above = bf16[2,128,512]{2,1,0:T(8,128)(2,1)} collective-permute-done((bf16[2,128,512]{2,1,0:T(8,128)(2,1)}, bf16[2,128,512]{2,1,0:T(8,128)(2,1)}, u32[]{:S(2)}, u32[]{:S(2)}) %collective-permute-start.3) | collective-permute-done | bytes 262176 | tf_op jit(solution)/shard_map/ppermute | solution.py:142
  50.4 0.0 copy-done.3
  50.4 11.7 %shard_map.111 = bf16[6,128,512]{2,1,0:T(8,128)(2,1)} custom-call(s32[6,4]{1,0:T(8,128)S(1)} %copy.12.ids, s32[6]{0:T(128)S(1)} %fusion.valid, bf16[6,128,512]{2,1,0:T(8,128)(2,1)S(1)} %bitcast.18, bf16[6,128,512]{2,1,0:T(8,128)(2,1)S(1)} %bitcast.20, bf16[6,128,512]{2,1,0:T(8,128)(2,1)S(1)} %bitcast.21, bf16[6,128,512]{2,1,0:T(8,128)(2,1)S(1)} %bitcast.22, ...), custom_call_target="tpu_custom_call" | custom-call | tf_op jit(solution)/shard_map/pallas_call | solution.py:181
  (2 shorter events, 0.0 us)
Async XLA Ops:
  0.0 22.9 %copy-start.8 = (s32[1,6,4]{1,2,0:T(4,128)S(1)}, s32[1,6,4]{1,2,0:T(4,128)}, u32[]{:S(2)}) copy-start(s32[1,6,4]{1,2,0:T(4,128)} %param.20) | copy-start | bytes 292
  0.0 44.3 %copy-start.9 = (s32[1,6]{1,0:T(1,128)S(1)}, s32[1,6]{1,0:T(1,128)}, u32[]{:S(2)}) copy-start(s32[1,6]{1,0:T(1,128)} %param.21) | copy-start | bytes 76
  0.0 44.4 %copy-start.1 = (bf16[512,512]{1,0:T(8,128)(2,1)S(1)}, bf16[512,512]{1,0:T(8,128)(2,1)}, u32[]{:S(2)}) copy-start(bf16[512,512]{1,0:T(8,128)(2,1)} %wk.3) | copy-start | bytes 1572868
  0.0 44.4 %copy-start.5 = (f32[512]{0:T(512)S(1)}, f32[512]{0:T(512)}, u32[]{:S(2)}) copy-start(f32[512]{0:T(512)} %param.19) | copy-start | bytes 6148
  0.0 44.4 %copy-start.7 = (f32[512]{0:T(512)S(1)}, f32[512]{0:T(512)}, u32[]{:S(2)}) copy-start(f32[512]{0:T(512)} %param.18) | copy-start | bytes 6148
  1.1 4.4 %collective-permute-start.1 = (bf16[1,128,512]{2,1,0:T(8,128)(2,1)S(1)}, bf16[1,128,512]{2,1,0:T(8,128)(2,1)S(1)}, u32[]{:S(2)}, u32[]{:S(2)}) collective-permute-start(bf16[1,128,512]{2,1,0:T(8,128)(2,1)S(1)} %get-tuple-element.13), channel_id=1, source_target_pairs={{1,0},{2,1},{3,2},{5,4},{6,5},{7,6},{9,8},{10,9},{11,10},{13,12},{... | collective-permute-start | bytes 393224 | tf_op jit(solution)/shard_map/ppermute | solution.py:143
  3.0 6.3 %collective-permute-start = (bf16[1,128,512]{2,1,0:T(8,128)(2,1)S(1)}, bf16[1,128,512]{2,1,0:T(8,128)(2,1)S(1)}, u32[]{:S(2)}, u32[]{:S(2)}) collective-permute-start(bf16[1,128,512]{2,1,0:T(8,128)(2,1)S(1)} %get-tuple-element.14), channel_id=1, source_target_pairs={{0,1},{1,2},{2,3},{4,5},{5,6},{6,7},{8,9},{9,10},{10,11},{12,13},{... | collective-permute-start | bytes 393224 | tf_op jit(solution)/shard_map/ppermute | solution.py:142
  9.3 1.1 %copy-start = (bf16[1,6,128,512]{3,2,1,0:T(8,128)(2,1)S(1)}, bf16[1,6,128,512]{3,2,1,0:T(8,128)(2,1)}, u32[]{:S(2)}) copy-start(bf16[1,6,128,512]{3,2,1,0:T(8,128)(2,1)} %param.11) | copy-start | bytes 2359300
  10.4 0.7 %copy-start.4 = (f32[512]{0:T(512)S(1)}, f32[512]{0:T(512)}, u32[]{:S(2)}) copy-start(f32[512]{0:T(512)} %param.13) | copy-start | bytes 6148
  11.1 33.3 %copy-start.2 = (bf16[512,512]{1,0:T(8,128)(2,1)S(1)}, bf16[512,512]{1,0:T(8,128)(2,1)}, u32[]{:S(2)}) copy-start(bf16[512,512]{1,0:T(8,128)(2,1)} %wv.3) | copy-start | bytes 1572868
  19.3 31.1 %copy-start.3 = (bf16[512,512]{1,0:T(8,128)(2,1)S(1)}, bf16[512,512]{1,0:T(8,128)(2,1)}, u32[]{:S(2)}) copy-start(bf16[512,512]{1,0:T(8,128)(2,1)} %wo.1) | copy-start | bytes 1572868
  19.3 19.8 %collective-permute-start.2 = (bf16[6,128,512]{2,1,0:T(8,128)(2,1)S(1)}, bf16[6,128,512]{2,1,0:T(8,128)(2,1)S(1)}, u32[]{:S(2)}, u32[]{:S(2)}) collective-permute-start(bf16[6,128,512]{2,1,0:T(8,128)(2,1)S(1)} %bitcast.17), channel_id=1, source_target_pairs={{0,4},{4,8},{8,12},{12,16},{16,20},{20,24},{24,28},{1,5},{5,9},{9,... | collective-permute-start | bytes 2359304 | tf_op jit(solution)/shard_map/ppermute | solution.py:164
  39.9 7.8 %collective-permute-start.4 = (bf16[2,128,512]{2,1,0:T(8,128)(2,1)}, bf16[2,128,512]{2,1,0:T(8,128)(2,1)S(1)}, u32[]{:S(2)}, u32[]{:S(2)}) collective-permute-start(bf16[2,128,512]{2,1,0:T(8,128)(2,1)} %get-tuple-element.11), channel_id=1, source_target_pairs={{1,0},{2,1},{3,2},{5,4},{6,5},{7,6},{9,8},{10,9},{11,10},{13,12},{... | collective-permute-start | bytes 786440 | tf_op jit(solution)/shard_map/ppermute | solution.py:143
  42.4 8.0 %collective-permute-start.3 = (bf16[2,128,512]{2,1,0:T(8,128)(2,1)}, bf16[2,128,512]{2,1,0:T(8,128)(2,1)}, u32[]{:S(2)}, u32[]{:S(2)}) collective-permute-start(bf16[2,128,512]{2,1,0:T(8,128)(2,1)} %get-tuple-element.12), channel_id=1, source_target_pairs={{0,1},{1,2},{2,3},{4,5},{5,6},{6,7},{8,9},{9,10},{10,11},{12,13},{... | collective-permute-start | bytes 786440 | tf_op jit(solution)/shard_map/ppermute | solution.py:142
  44.5 1.0 %copy-start.6 = (bf16[512,512]{1,0:T(8,128)(2,1)S(1)}, bf16[512,512]{1,0:T(8,128)(2,1)}, u32[]{:S(2)}) copy-start(bf16[512,512]{1,0:T(8,128)(2,1)} %wq.1) | copy-start | bytes 1572868

commit v2 on v1

v2 whole, which is shorter than its diff:
```python
import functools

import jax
import jax.numpy as jnp
from jax import lax
from jax.experimental import pallas as pl
from jax.experimental.pallas import tpu as pltpu
from jax.sharding import PartitionSpec as P

HEADS = 8
HD = 64
KSRC = 4
DISP = 2
GROUP = 4
F32 = jnp.float32
BF16 = jnp.bfloat16


def dot(a, b):
    return jnp.dot(a, b, preferred_element_type=F32)


def shift_columns(left, mid, right, width):
    count = mid.shape[0]
    col = lax.broadcasted_iota(jnp.int32, mid.shape, 0) % width
    return (
        mid
        + jnp.where(col == 0, 0.0, pltpu.roll(left, 1, 0))
        + jnp.where(col == width - 1, 0.0, pltpu.roll(right, count - 1, 0))
    )


def head_mean(chans):
    row = lax.broadcasted_iota(jnp.int32, (chans, chans), 0) // HD
    col = lax.broadcasted_iota(jnp.int32, (chans, chans), 1) // HD
    return jnp.where(row == col, 1.0 / HD, 0.0).astype(BF16)


def normed(feats, weight, gain, mean, scale):
    proj = dot(feats, weight)
    square = dot((proj * proj).astype(BF16), mean)
    out = (proj * lax.rsqrt(square + 1e-06) * gain).astype(BF16)
    return out * scale if scale != 1 else out


def kernel(
    ids, valid, x, wc_hbm, wq_hbm, wk_hbm, wv_hbm, wo_hbm, bias, gq, gk,
    out,
    ext, wc, wq, wk, wv, wo, feats, reach, q, keys, values, mixed,
    local_sem, send_sem, recv_sem,
):
    rows, width, chans = x.shape
    frame, band = lax.axis_index("frame"), lax.axis_index("row")
    frames, bands = lax.axis_size("frame"), lax.axis_size("row")
    has_prev, has_next = frame > 0, frame < frames - 1
    has_above, has_below = band > 0, band < bands - 1
    to_above, to_below, to_next = {"row": band - 1}, {"row": band + 1}, {"frame": frame + 1}

    def fetch(i, src, dst):
        return pltpu.make_async_copy(src, dst, local_sem.at[i])

    def send(i, src, dst, device):
        return pltpu.make_async_remote_copy(
            src_ref=src,
            dst_ref=dst,
            send_sem=send_sem.at[i],
            recv_sem=recv_sem.at[i],
            device_id=device,
            device_id_type=pl.DeviceIdType.MESH,
        )

    load_x = fetch(0, x, ext.at[pl.ds(1, rows)])
    load_x.start()
    taps = [fetch(1 + b, wc_hbm.at[:, b], wc.at[:, b]) for b in range(3)]
    mats = [
        fetch(4 + i, src, dst)
        for i, (src, dst) in enumerate(
            ((wq_hbm, wq), (wk_hbm, wk), (wv_hbm, wv), (wo_hbm, wo))
        )
    ]
    for copy in taps + mats:
        copy.start()

    barrier = pltpu.get_barrier_semaphore()
    met = 0
    for there, device in (
        (has_above, to_above),
        (has_below, to_below),
        (has_prev, {"frame": frame - 1}),
        (has_next, to_next),
    ):
        met = met + there.astype(jnp.int32)

        @pl.when(there)
        def _():
            pl.semaphore_signal(
                barrier, inc=1, device_id=device, device_id_type=pl.DeviceIdType.MESH
            )

    pl.semaphore_wait(barrier, met)

    halo_up = send(0, x.at[0], ext.at[rows + 1], to_above)
    halo_down = send(1, x.at[rows - 1], ext.at[0], to_below)

    @pl.when(has_above)
    def _():
        halo_up.start()

    @pl.when(has_below)
    def _():
        halo_down.start()

    blank = jnp.zeros((width, chans), BF16)

    @pl.when(band == 0)
    def _():
        ext[0] = blank
        for i in range(DISP):
            reach[i] = blank

    @pl.when(band == bands - 1)
    def _():
        ext[rows + 1] = blank
        for i in range(DISP):
            reach[DISP + rows + i] = blank

    @pl.when(frame == 0)
    def _():
        for i in range(rows + 2 * DISP):
            reach[i] = blank

    spans = ((0, DISP), (rows - DISP, DISP), (DISP, rows - 2 * DISP))
    moves = [
        send(
            2 + i,
            feats.at[pl.ds(start, size)],
            reach.at[pl.ds(DISP + start, size)],
            to_next,
        )
        for i, (start, size) in enumerate(spans)
    ]
    relay_up = send(5, reach.at[pl.ds(DISP, DISP)], reach.at[pl.ds(DISP + rows, DISP)], to_above)
    relay_down = send(6, reach.at[pl.ds(rows, DISP)], reach.at[pl.ds(0, DISP)], to_below)

    load_x.wait()
    for i, (start, size) in enumerate(spans):
        if i == 0:

            @pl.when(has_above)
            def _():
                halo_down.wait_recv()

        if i == 1:

            @pl.when(has_below)
            def _():
                halo_up.wait_recv()

        window = jnp.concatenate(
            [ext[start + a : start + a + size].reshape(size * width, chans) for a in range(3)],
            axis=1,
        )
        parts = []
        for b in range(3):
            if i == 0:
                taps[b].wait()
            parts.append(dot(window, jnp.concatenate([wc[a, b] for a in range(3)], axis=0)))
        total = shift_columns(*parts, width) + bias[...]
        feats[start : start + size] = total.astype(BF16).reshape(size, width, chans)

        @pl.when(has_next)
        def _():
            moves[i].start()

    mean = head_mean(chans)

    def project(src, start, size, place):
        f = src[start : start + size].reshape(size * width, chans)
        blocked = (size, width, chans)
        keys[place : place + size] = normed(f, wk[...], gk[...], mean, 1).reshape(blocked)
        values[place : place + size] = dot(f, wv[...]).astype(BF16).reshape(blocked)

    for copy in mats:
        copy.wait()
    flat = feats[...].reshape(rows * width, chans)
    q[...] = normed(flat, wq[...], gq[...], mean, HD**-0.5).reshape(rows, width, chans)
    project(feats, 0, rows, 0)

    @pl.when(has_prev)
    def _():
        moves[0].wait_recv()

    @pl.when(has_prev & has_above)
    def _():
        relay_up.start()

    project(reach, DISP, DISP, rows + DISP)

    @pl.when(has_prev)
    def _():
        moves[1].wait_recv()

    @pl.when(has_prev & has_below)
    def _():
        relay_down.start()

    project(reach, rows, DISP, 2 * rows)

    @pl.when(has_prev & has_above)
    def _():
        relay_down.wait_recv()

    project(reach, 0, DISP, rows)

    @pl.when(has_prev & has_below)
    def _():
        relay_up.wait_recv()

    project(reach, DISP + rows, DISP, 2 * rows + DISP)

    @pl.when(has_prev)
    def _():
        moves[2].wait_recv()

    project(reach, 2 * DISP, rows - 2 * DISP, rows + 2 * DISP)

    lanes = GROUP * HD
    head = lax.broadcasted_iota(jnp.int32, (1, lanes), 1) // HD
    slot = lax.broadcasted_iota(jnp.int32, (1, (1 + KSRC) * width), 1) // width
    base = band * rows - DISP - rows
    live = has_prev.astype(jnp.int32)

    def block(n, carry):
        places = [n] + [
            jnp.clip(ids[0, n, j] - base, rows, 2 * rows + 2 * DISP - 1) for j in range(KSRC)
        ]
        mask = slot <= valid[0, n] * live
        for g in range(chans // lanes):
            cut = pl.ds(g * lanes, lanes)
            key = jnp.concatenate([keys[p, :, cut] for p in places], axis=0)
            value = jnp.concatenate([values[p, :, cut] for p in places], axis=0)
            query = q[n, :, cut]
            stack = jnp.concatenate(
                [jnp.where(head == h, query, jnp.zeros_like(query)) for h in range(GROUP)], axis=0
            )
            scores = lax.dot_general(
                stack, key, (((1,), (1,)), ((), ())), preferred_element_type=F32
            )
            expo = jnp.where(mask, jnp.exp(scores), 0.0)
            total = jnp.sum(expo, axis=1, keepdims=True)
            part = dot(expo.astype(BF16), value) / total
            joined = part[0:width]
            for h in range(1, GROUP):
                joined = jnp.where(head == h, part[h * width : (h + 1) * width], joined)
            mixed[n, :, cut] = joined.astype(BF16)
        return carry

    lax.fori_loop(0, rows, block, 0)
    flat = mixed[...].reshape(rows * width, chans)
    f = feats[...].reshape(rows * width, chans).astype(F32)
    out[...] = (f + dot(flat, wo[...])).astype(BF16).reshape(rows, width, chans)

    @pl.when(has_above)
    def _():
        halo_up.wait_send()

    @pl.when(has_below)
    def _():
        halo_down.wait_send()

    for copy in moves:

        @pl.when(has_next)
        def _():
            copy.wait_send()

    @pl.when(has_prev & has_above)
    def _():
        relay_up.wait_send()

    @pl.when(has_prev & has_below)
    def _():
        relay_down.wait_send()


VM = pl.BlockSpec(memory_space=pltpu.VMEM)
SM = pl.BlockSpec(memory_space=pltpu.SMEM)
ANY = pl.BlockSpec(memory_space=pl.ANY)


def shards(x, wc, bias, wq, wk, wv, wo, gq, gk, source_ids, valid_counts):
    x = x[0]
    rows, width, chans = x.shape
    square = pltpu.VMEM((chans, chans), BF16)

    def stack(count):
        return pltpu.VMEM((count, width, chans), BF16)

    out = pl.pallas_call(
        kernel,
        out_shape=jax.ShapeDtypeStruct((rows, width, chans), BF16),
        in_specs=[SM, SM] + [ANY] * 6 + [VM] * 3,
        out_specs=VM,
        scratch_shapes=[
            stack(rows + 2),
            pltpu.VMEM(wc.shape, BF16),
            square,
            square,
            square,
            square,
            stack(rows),
            stack(rows + 2 * DISP),
            stack(rows),
            stack(2 * rows + 2 * DISP),
            stack(2 * rows + 2 * DISP),
            stack(rows),
            pltpu.SemaphoreType.DMA((8,)),
            pltpu.SemaphoreType.DMA((7,)),
            pltpu.SemaphoreType.DMA((7,)),
        ],
        compiler_params=pltpu.CompilerParams(
            vmem_limit_bytes=56 * 2**20, collective_id=0, has_side_effects=True
        ),
    )(source_ids, valid_counts, x, wc, wq, wk, wv, wo, bias[None], gq[None], gk[None])
    return out[None]


def solution(mesh):
    return jax.shard_map(
        shards,
        mesh=mesh,
        in_specs=(P("frame", "row", None, None),)
        + (P(),) * 8
        + (P("frame", "row", None), P("frame", "row")),
        out_specs=P("frame", "row", None, None),
        check_vma=False,
    )
```

time: 62.5 us -> 37.7 us (0.60)
  waiting for transfers between devices: 22.8 us -> 0 us
  starting transfers between devices: 12.3 us -> 0 us
  Pallas kernels: 22.1 us -> 34 us
  local copies, waits for them, and re-layouts: 4.83 us -> 3.45 us
    ppermute x5 -> x0, waiting for transfers between devices: 22.8 us -> none  [the longest x1 16.2 us: shards(): lax.ppermute(feats.reshape(rows, width, chans), 'frame', [(i, i + 1) for...]
    ppermute x5 -> x0, starting transfers between devices: 12.3 us -> none  [the longest x2 4.38 us: edges(): after = lax.ppermute(block[:width], 'row', down)]
    pallas_call x3 -> x1, Pallas kernels: 22.1 us -> 34 us  [shards(): pl.pallas_call(kernel, out_shape=jax.ShapeDtypeStruct((rows, width, chans...]
    slice x2 -> x0, local copies, waits for them, and re-layouts: 1.86 us -> none  [edges(): after = lax.ppermute(block[:width], 'row', down)]
    unnamed x20 -> x2, local copies, waits for them, and re-layouts: 2.88 us -> 3.45 us
  transfers between devices with their start and end apart: 5 -> 0, of which waited for: 4 -> 0; matrix products, arithmetic and copies ran while one was open for 0% -> 0% of each run, Pallas kernels for 4% -> 0%
where the time goes in v2:
time: 37.7 us; the launch traced here: 37.4 us
  Pallas kernels  34 us (90%)
  local copies, waits for them, and re-layouts  3.45 us (9%)
    pallas_call x1, Pallas kernels, shards(): pl.pallas_call(kernel, out_shape=jax.ShapeDtypeStruct((rows, width, chans...  34 us
    unnamed x2, local copies, waits for them, and re-layouts  3.45 us

profile of v2, /device:TPU:26, one launch (start us, length us, event | category | flops | bytes accessed | tf_op | source)
XLA Modules:
  0.0 37.4 jit_solution(15466868682958444766)
XLA Ops:
  0.0 1.4 %copy.12.ids = s32[1,6,4]{2,1,0:T(8,128)} copy(s32[1,6,4]{1,2,0:T(4,128)} %param.20) | data formatting | bytes 192 | tf_op args[9]
  1.4 34.0 %shard_map.109 = bf16[6,128,512]{2,1,0:T(8,128)(2,1)} custom-call(s32[1,6,4]{2,1,0:T(8,128)} %copy.12.ids, s32[1,6]{1,0:T(1,128)} %valid.1, bf16[6,128,512]{2,1,0:T(8,128)(2,1)} %bitcast.6, bf16[3,3,512,512]{3,2,1,0:T(8,128)(2,1)} %wc_hbm.1, bf16[512,512]{1,0:T(8,128)(2,1)} %wq_hbm.1, bf16[512,512]{1,0:T(8,128)(2,1)} %wk_hbm.1, bf16[512,512]{1,0:T(8,128)(2,1)} %wv_hbm.1, ...), custom_call_target="tpu_custom_call" | custom-call | tf_op jit(solution)/shard_map/pallas_call | solution.py:299
  35.3 2.1 %copy.14 = bf16[1,6,128,512]{3,2,1,0:T(8,128)(2,1)} copy(bf16[1,6,128,512]{3,2,1,0:T(8,128)(2,1)} %bitcast.5) | data formatting | bytes 1572864

commit v3 on v2

--- a/solution.py
+++ b/solution.py
@@ -44,9 +44,9 @@
 
 
 def kernel(
-    ids, valid, x, wc_hbm, wq_hbm, wk_hbm, wv_hbm, wo_hbm, bias, gq, gk,
-    out,
-    ext, wc, wq, wk, wv, wo, feats, reach, q, keys, values, mixed,
+    ids, valid, x, wc_hbm, wq_hbm, wk_hbm, wv_hbm, bias, gq, gk,
+    feats, mixed,
+    ext, wc, wq, wk, wv, reach, q, keys, values, mixture, sums,
     local_sem, send_sem, recv_sem,
 ):
     rows, width, chans = x.shape
@@ -75,7 +75,7 @@
     mats = [
         fetch(4 + i, src, dst)
         for i, (src, dst) in enumerate(
-            ((wq_hbm, wq), (wk_hbm, wk), (wv_hbm, wv), (wo_hbm, wo))
+            ((wq_hbm, wq), (wk_hbm, wk), (wv_hbm, wv))
         )
     ]
     for copy in taps + mats:
@@ -180,11 +180,74 @@
         keys[place : place + size] = normed(f, wk[...], gk[...], mean, 1).reshape(blocked)
         values[place : place + size] = dot(f, wv[...]).astype(BF16).reshape(blocked)
 
+    lanes = GROUP * HD
+    head = lax.broadcasted_iota(jnp.int32, (1, lanes), 1) // HD
+    base = band * rows - DISP
+    live = has_prev.astype(jnp.int32)
+
+    def by_head(stacked):
+        joined = stacked[0:width]
+        for h in range(1, GROUP):
+            joined = jnp.where(head == h, stacked[h * width : (h + 1) * width], joined)
+        return joined
+
+    def times(n, row):
+        limit = valid[0, n] * live
+        found = 0
+        for j in range(KSRC):
+            found += ((ids[0, j, n] - base == row) & (j < limit)).astype(jnp.int32)
+        return found.astype(F32)
+
+    def attend(first, last, place, size, row):
+        which = lax.broadcasted_iota(jnp.int32, (1, size * width), 1) // width
+
+        def block(n, carry):
+            if row is not None:
+                weight = jnp.zeros((1, size * width), F32)
+                for i in range(size):
+                    weight = jnp.where(which == i, times(n, row + i), weight)
+            for g in range(chans // lanes):
+                cut = pl.ds(g * lanes, lanes)
+                spot = pl.ds(n if row is None else place, size)
+                key = keys[spot, :, cut].reshape(size * width, lanes)
+                value = values[spot, :, cut].reshape(size * width, lanes)
+                query = q[n, :, cut]
+                stack = jnp.concatenate(
+                    [jnp.where(head == h, query, jnp.zeros_like(query)) for h in range(GROUP)],
+                    axis=0,
+                )
+                scores = lax.dot_general(
+                    stack, key, (((1,), (1,)), ((), ())), preferred_element_type=F32
+                )
+                expo = jnp.exp(scores)
+                if row is not None:
+                    expo = expo * weight
+                folded = expo[:, 0:width]
+                for i in range(1, size):
+                    folded = folded + expo[:, i * width : (i + 1) * width]
+                part = by_head(dot(expo.astype(BF16), value))
+                if row is None:
+                    sums[n, g] = folded
+                    mixture[n, :, cut] = part
+                else:
+                    sums[n, g] += folded
+                    mixture[n, :, cut] += part
+            return carry
+
+        lax.fori_loop(first, last, block, 0)
+
+    def meet(start, size):
+        project(reach, start, size, rows + start)
+        first = max(0, start - 2 * DISP)
+        last = min(rows, start + size)
+        attend(first, last, rows + start, size, start)
+
     for copy in mats:
         copy.wait()
     flat = feats[...].reshape(rows * width, chans)
     q[...] = normed(flat, wq[...], gq[...], mean, HD**-0.5).reshape(rows, width, chans)
     project(feats, 0, rows, 0)
+    attend(0, rows, None, 1, None)
 
     @pl.when(has_prev)
     def _():
@@ -194,7 +257,7 @@
     def _():
         relay_up.start()
 
-    project(reach, DISP, DISP, rows + DISP)
+    meet(DISP, DISP)
 
     @pl.when(has_prev)
     def _():
@@ -204,61 +267,34 @@
     def _():
         relay_down.start()
 
-    project(reach, rows, DISP, 2 * rows)
+    meet(rows, DISP)
 
     @pl.when(has_prev & has_above)
     def _():
         relay_down.wait_recv()
 
-    project(reach, 0, DISP, rows)
+    meet(0, DISP)
 
     @pl.when(has_prev & has_below)
     def _():
         relay_up.wait_recv()
 
-    project(reach, DISP + rows, DISP, 2 * rows + DISP)
+    meet(DISP + rows, DISP)
 
     @pl.when(has_prev)
     def _():
         moves[2].wait_recv()
 
-    project(reach, 2 * DISP, rows - 2 * DISP, rows + 2 * DISP)
-
-    lanes = GROUP * HD
-    head = lax.broadcasted_iota(jnp.int32, (1, lanes), 1) // HD
-    slot = lax.broadcasted_iota(jnp.int32, (1, (1 + KSRC) * width), 1) // width
-    base = band * rows - DISP - rows
-    live = has_prev.astype(jnp.int32)
-
-    def block(n, carry):
-        places = [n] + [
-            jnp.clip(ids[0, n, j] - base, rows, 2 * rows + 2 * DISP - 1) for j in range(KSRC)
-        ]
-        mask = slot <= valid[0, n] * live
+    meet(2 * DISP, rows - 2 * DISP)
+
+    def finish(n, carry):
         for g in range(chans // lanes):
             cut = pl.ds(g * lanes, lanes)
-            key = jnp.concatenate([keys[p, :, cut] for p in places], axis=0)
-            value = jnp.concatenate([values[p, :, cut] for p in places], axis=0)
-            query = q[n, :, cut]
-            stack = jnp.concatenate(
-                [jnp.where(head == h, query, jnp.zeros_like(query)) for h in range(GROUP)], axis=0
-            )
-            scores = lax.dot_general(
-                stack, key, (((1,), (1,)), ((), ())), preferred_element_type=F32
-            )
-            expo = jnp.where(mask, jnp.exp(scores), 0.0)
-            total = jnp.sum(expo, axis=1, keepdims=True)
-            part = dot(expo.astype(BF16), value) / total
-            joined = part[0:width]
-            for h in range(1, GROUP):
-                joined = jnp.where(head == h, part[h * width : (h + 1) * width], joined)
-            mixed[n, :, cut] = joined.astype(BF16)
+            inverse = 1.0 / jnp.sum(sums[n, g], axis=1, keepdims=True)
+            mixed[n, :, cut] = (mixture[n, :, cut] * by_head(inverse)).astype(BF16)
         return carry
 
-    lax.fori_loop(0, rows, block, 0)
-    flat = mixed[...].reshape(rows * width, chans)
-    f = feats[...].reshape(rows * width, chans).astype(F32)
-    out[...] = (f + dot(flat, wo[...])).astype(BF16).reshape(rows, width, chans)
+    lax.fori_loop(0, rows, finish, 0)
 
     @pl.when(has_above)
     def _():
@@ -296,24 +332,24 @@
     def stack(count):
         return pltpu.VMEM((count, width, chans), BF16)
 
-    out = pl.pallas_call(
+    block = jax.ShapeDtypeStruct((rows, width, chans), BF16)
+    feats, mixed = pl.pallas_call(
         kernel,
-        out_shape=jax.ShapeDtypeStruct((rows, width, chans), BF16),
-        in_specs=[SM, SM] + [ANY] * 6 + [VM] * 3,
-        out_specs=VM,
+        out_shape=(block, block),
+        in_specs=[SM, SM] + [ANY] * 5 + [VM] * 3,
+        out_specs=(VM, VM),
         scratch_shapes=[
             stack(rows + 2),
             pltpu.VMEM(wc.shape, BF16),
             square,
             square,
             square,
-            square,
-            stack(rows),
             stack(rows + 2 * DISP),
             stack(rows),
             stack(2 * rows + 2 * DISP),
             stack(2 * rows + 2 * DISP),
-            stack(rows),
+            pltpu.VMEM((rows, width, chans), F32),
+            pltpu.VMEM((rows, chans // (GROUP * HD), GROUP * width, width), F32),
             pltpu.SemaphoreType.DMA((8,)),
             pltpu.SemaphoreType.DMA((7,)),
             pltpu.SemaphoreType.DMA((7,)),
@@ -321,8 +357,10 @@
         compiler_params=pltpu.CompilerParams(
             vmem_limit_bytes=56 * 2**20, collective_id=0, has_side_effects=True
         ),
-    )(source_ids, valid_counts, x, wc, wq, wk, wv, wo, bias[None], gq[None], gk[None])
-    return out[None]
+    )(jnp.swapaxes(source_ids, 1, 2), valid_counts, x, wc, wq, wk, wv, bias[None], gq[None], gk[None])
+    mixed, feats = mixed.reshape(rows * width, chans), feats.reshape(rows * width, chans)
+    out = (feats.astype(F32) + dot(mixed, wo)).astype(BF16)
+    return out.reshape(1, rows, width, chans)
 
 
 def solution(mesh):

time: 37.7 us -> 39.4 us (1.045)
  local copies, waits for them, and re-layouts: 3.45 us -> 0.01 us
  matrix products: 0 us -> 2.82 us
  Pallas kernels: 34 us -> 36.4 us
    unnamed x2, local copies, waits for them, and re-layouts: 3.45 us -> 0.01 us
    dot_general x0 -> x1, matrix products: none -> 2.82 us  [dot(): return jnp.dot(a, b, preferred_element_type=F32)]
    pallas_call x1, Pallas kernels: 34 us -> 36.4 us  [shards(): pl.pallas_call(kernel, out_shape=(block, block), in_specs=[SM, SM] + [ANY...]
where the time goes in v3:
time: 39.4 us; the launch traced here: 39.3 us
  Pallas kernels  36.4 us (92%)
  matrix products  2.82 us (7%)
    pallas_call x1, Pallas kernels, shards(): pl.pallas_call(kernel, out_shape=(block, block), in_specs=[SM, SM] + [ANY...  36.4 us
    dot_general x1, matrix products, dot(): return jnp.dot(a, b, preferred_element_type=F32)  2.82 us

profile of v3, /device:TPU:26, one launch (start us, length us, event | category | flops | bytes accessed | tf_op | source)
XLA Modules:
  0.0 39.3 jit_solution(14962217956024492673)
XLA Ops:
  0.0 0.0 copy-start
  0.0 36.4 %shard_map.109 = (bf16[6,128,512]{2,1,0:T(8,128)(2,1)}, bf16[6,128,512]{2,1,0:T(8,128)(2,1)}) custom-call(s32[1,4,6]{2,1,0:T(4,128)} %bitcast.12, s32[1,6]{1,0:T(1,128)} %valid.1, bf16[6,128,512]{2,1,0:T(8,128)(2,1)} %bitcast.11, bf16[3,3,512,512]{3,2,1,0:T(8,128)(2,1)} %wc_hbm.1, bf16[512,512]{1,0:T(8,128)(2,1)} %wq_hbm.1, bf16[512,512]{1,0:T(8,128)(2,1)} %wk_hbm.1, ...), custom_call_target="tpu_custom_call" | custom-call | tf_op jit(solution)/shard_map/pallas_call | solution.py:336
  36.5 0.0 copy-done
  36.5 2.8 %fusion = bf16[768,512]{1,0:T(8,128)(2,1)} fusion(bf16[768,512]{1,0:T(8,128)(2,1)} %bitcast.16, bf16[768,512]{1,0:T(8,128)(2,1)} %bitcast.17, bf16[512,512]{1,0:T(8,128)(2,1)S(1)} %copy-done), kind=kOutput, calls=%fused_computation.1 | convolution fusion | flops 403832832 | bytes 2883584 | tf_op jit(solution)/shard_map/dot_general | solution.py:20
Async XLA Ops:
  0.0 36.5 %copy-start = (bf16[512,512]{1,0:T(8,128)(2,1)S(1)}, bf16[512,512]{1,0:T(8,128)(2,1)}, u32[]{:S(2)}) copy-start(bf16[512,512]{1,0:T(8,128)(2,1)} %param.17) | copy-start | bytes 1572868

commit v4 on v2

--- a/solution.py
+++ b/solution.py
@@ -46,7 +46,7 @@
 def kernel(
     ids, valid, x, wc_hbm, wq_hbm, wk_hbm, wv_hbm, wo_hbm, bias, gq, gk,
     out,
-    ext, wc, wq, wk, wv, wo, feats, reach, q, keys, values, mixed,
+    ext, wc, wq, wk, wv, wo, feats, reach, q, keys, values, mixed, mixture, sums,
     local_sem, send_sem, recv_sem,
 ):
     rows, width, chans = x.shape
@@ -180,6 +180,53 @@
         keys[place : place + size] = normed(f, wk[...], gk[...], mean, 1).reshape(blocked)
         values[place : place + size] = dot(f, wv[...]).astype(BF16).reshape(blocked)
 
+    lanes = GROUP * HD
+    head = lax.broadcasted_iota(jnp.int32, (1, lanes), 1) // HD
+    slot = lax.broadcasted_iota(jnp.int32, (1, KSRC * width), 1) // width
+    base = band * rows - DISP - rows
+    live = has_prev.astype(jnp.int32)
+
+    def by_head(stacked):
+        joined = stacked[0:width]
+        for h in range(1, GROUP):
+            joined = jnp.where(head == h, stacked[h * width : (h + 1) * width], joined)
+        return joined
+
+    def exponentials(n, cut, key):
+        query = q[n, :, cut]
+        stack = jnp.concatenate(
+            [jnp.where(head == h, query, jnp.zeros_like(query)) for h in range(GROUP)], axis=0
+        )
+        return jnp.exp(
+            lax.dot_general(stack, key, (((1,), (1,)), ((), ())), preferred_element_type=F32)
+        )
+
+    def own(n, carry):
+        for g in range(chans // lanes):
+            cut = pl.ds(g * lanes, lanes)
+            expo = exponentials(n, cut, keys[n, :, cut])
+            sums[n, g] = expo
+            mixture[n, :, cut] = by_head(dot(expo.astype(BF16), values[n, :, cut]))
+        return carry
+
+    def block(n, carry):
+        places = [
+            jnp.clip(ids[0, j, n] - base, rows, 2 * rows + 2 * DISP - 1) for j in range(KSRC)
+        ]
+        mask = slot < valid[0, n] * live
+        for g in range(chans // lanes):
+            cut = pl.ds(g * lanes, lanes)
+            key = jnp.concatenate([keys[p, :, cut] for p in places], axis=0)
+            value = jnp.concatenate([values[p, :, cut] for p in places], axis=0)
+            expo = jnp.where(mask, exponentials(n, cut, key), 0.0)
+            folded = sums[n, g]
+            for j in range(KSRC):
+                folded = folded + expo[:, j * width : (j + 1) * width]
+            inverse = 1.0 / jnp.sum(folded, axis=1, keepdims=True)
+            part = by_head(dot(expo.astype(BF16), value)) + mixture[n, :, cut]
+            mixed[n, :, cut] = (part * by_head(inverse)).astype(BF16)
+        return carry
+
     for copy in mats:
         copy.wait()
     flat = feats[...].reshape(rows * width, chans)
@@ -195,6 +242,7 @@
         relay_up.start()
 
     project(reach, DISP, DISP, rows + DISP)
+    lax.fori_loop(0, rows, own, 0)
 
     @pl.when(has_prev)
     def _():
@@ -223,37 +271,6 @@
         moves[2].wait_recv()
 
     project(reach, 2 * DISP, rows - 2 * DISP, rows + 2 * DISP)
-
-    lanes = GROUP * HD
-    head = lax.broadcasted_iota(jnp.int32, (1, lanes), 1) // HD
-    slot = lax.broadcasted_iota(jnp.int32, (1, (1 + KSRC) * width), 1) // width
-    base = band * rows - DISP - rows
-    live = has_prev.astype(jnp.int32)
-
-    def block(n, carry):
-        places = [n] + [
-            jnp.clip(ids[0, n, j] - base, rows, 2 * rows + 2 * DISP - 1) for j in range(KSRC)
-        ]
-        mask = slot <= valid[0, n] * live
-        for g in range(chans // lanes):
-            cut = pl.ds(g * lanes, lanes)
-            key = jnp.concatenate([keys[p, :, cut] for p in places], axis=0)
-            value = jnp.concatenate([values[p, :, cut] for p in places], axis=0)
-            query = q[n, :, cut]
-            stack = jnp.concatenate(
-                [jnp.where(head == h, query, jnp.zeros_like(query)) for h in range(GROUP)], axis=0
-            )
-            scores = lax.dot_general(
-                stack, key, (((1,), (1,)), ((), ())), preferred_element_type=F32
-            )
-            expo = jnp.where(mask, jnp.exp(scores), 0.0)
-            total = jnp.sum(expo, axis=1, keepdims=True)
-            part = dot(expo.astype(BF16), value) / total
-            joined = part[0:width]
-            for h in range(1, GROUP):
-                joined = jnp.where(head == h, part[h * width : (h + 1) * width], joined)
-            mixed[n, :, cut] = joined.astype(BF16)
-        return carry
 
     lax.fori_loop(0, rows, block, 0)
     flat = mixed[...].reshape(rows * width, chans)
@@ -314,6 +331,8 @@
             stack(2 * rows + 2 * DISP),
             stack(2 * rows + 2 * DISP),
             stack(rows),
+            pltpu.VMEM((rows, width, chans), F32),
+            pltpu.VMEM((rows, chans // (GROUP * HD), GROUP * width, width), F32),
             pltpu.SemaphoreType.DMA((8,)),
             pltpu.SemaphoreType.DMA((7,)),
             pltpu.SemaphoreType.DMA((7,)),
@@ -321,7 +340,7 @@
         compiler_params=pltpu.CompilerParams(
             vmem_limit_bytes=56 * 2**20, collective_id=0, has_side_effects=True
         ),
-    )(source_ids, valid_counts, x, wc, wq, wk, wv, wo, bias[None], gq[None], gk[None])
+    )(jnp.swapaxes(source_ids, 1, 2), valid_counts, x, wc, wq, wk, wv, wo, bias[None], gq[None], gk[None])
     return out[None]
 
 

time: 37.7 us -> 34.6 us (0.918)
  Pallas kernels: 34 us -> 32.4 us
  local copies, waits for them, and re-layouts: 3.45 us -> 2.1 us
    pallas_call x1, Pallas kernels: 34 us -> 32.4 us  [shards(): pl.pallas_call(kernel, out_shape=jax.ShapeDtypeStruct((rows, width, chans...]
    unnamed x2 -> x1, local copies, waits for them, and re-layouts: 3.45 us -> 2.1 us
where the time goes in v4:
time: 34.6 us; the launch traced here: 34.5 us
  Pallas kernels  32.4 us (94%)
  local copies, waits for them, and re-layouts  2.1 us (6%)
    pallas_call x1, Pallas kernels, shards(): pl.pallas_call(kernel, out_shape=jax.ShapeDtypeStruct((rows, width, chans...  32.4 us
    unnamed x1, local copies, waits for them, and re-layouts  2.1 us

profile of v4, /device:TPU:26, one launch (start us, length us, event | category | flops | bytes accessed | tf_op | source)
XLA Modules:
  0.0 34.5 jit_solution(14041981124366765591)
XLA Ops:
  0.0 32.4 %shard_map.109 = bf16[6,128,512]{2,1,0:T(8,128)(2,1)} custom-call(s32[1,4,6]{2,1,0:T(4,128)} %bitcast.8, s32[1,6]{1,0:T(1,128)} %valid.1, bf16[6,128,512]{2,1,0:T(8,128)(2,1)} %bitcast.7, bf16[3,3,512,512]{3,2,1,0:T(8,128)(2,1)} %wc_hbm.1, bf16[512,512]{1,0:T(8,128)(2,1)} %wq_hbm.1, bf16[512,512]{1,0:T(8,128)(2,1)} %wk_hbm.1, bf16[512,512]{1,0:T(8,128)(2,1)} %wv_hbm.1, ...), custom_call_target="tpu_custom_call" | custom-call | tf_op jit(solution)/shard_map/pallas_call | solution.py:316
  32.4 2.1 %copy.13 = bf16[1,6,128,512]{3,2,1,0:T(8,128)(2,1)} copy(bf16[1,6,128,512]{3,2,1,0:T(8,128)(2,1)} %bitcast.6) | data formatting | bytes 1572864

commit v5 on v4

--- a/solution.py
+++ b/solution.py
@@ -242,7 +242,7 @@
         relay_up.start()
 
     project(reach, DISP, DISP, rows + DISP)
-    lax.fori_loop(0, rows, own, 0)
+    lax.fori_loop(0, rows, own, 0, unroll=True)
 
     @pl.when(has_prev)
     def _():
@@ -272,7 +272,7 @@
 
     project(reach, 2 * DISP, rows - 2 * DISP, rows + 2 * DISP)
 
-    lax.fori_loop(0, rows, block, 0)
+    lax.fori_loop(0, rows, block, 0, unroll=True)
     flat = mixed[...].reshape(rows * width, chans)
     f = feats[...].reshape(rows * width, chans).astype(F32)
     out[...] = (f + dot(flat, wo[...])).astype(BF16).reshape(rows, width, chans)

time: 34.6 us -> 33.3 us (0.962)
  Pallas kernels: 32.4 us -> 31 us
    pallas_call x1, Pallas kernels: 32.4 us -> 31 us  [shards(): pl.pallas_call(kernel, out_shape=jax.ShapeDtypeStruct((rows, width, chans...]
where the time goes in v5:
time: 33.3 us; the launch traced here: 33.1 us
  Pallas kernels  31 us (93%)
  local copies, waits for them, and re-layouts  2.1 us (6%)
    pallas_call x1, Pallas kernels, shards(): pl.pallas_call(kernel, out_shape=jax.ShapeDtypeStruct((rows, width, chans...  31 us
    unnamed x1, local copies, waits for them, and re-layouts  2.1 us

profile of v5, /device:TPU:26, one launch (start us, length us, event | category | flops | bytes accessed | tf_op | source)
XLA Modules:
  0.0 33.1 jit_solution(14278512898293661510)
XLA Ops:
  0.0 31.0 %shard_map.109 = bf16[6,128,512]{2,1,0:T(8,128)(2,1)} custom-call(s32[1,4,6]{2,1,0:T(4,128)} %bitcast.8, s32[1,6]{1,0:T(1,128)} %valid.1, bf16[6,128,512]{2,1,0:T(8,128)(2,1)} %bitcast.7, bf16[3,3,512,512]{3,2,1,0:T(8,128)(2,1)} %wc_hbm.1, bf16[512,512]{1,0:T(8,128)(2,1)} %wq_hbm.1, bf16[512,512]{1,0:T(8,128)(2,1)} %wk_hbm.1, bf16[512,512]{1,0:T(8,128)(2,1)} %wv_hbm.1, ...), custom_call_target="tpu_custom_call" | custom-call | tf_op jit(solution)/shard_map/pallas_call | solution.py:316
  31.0 2.1 %copy.13 = bf16[1,6,128,512]{3,2,1,0:T(8,128)(2,1)} copy(bf16[1,6,128,512]{3,2,1,0:T(8,128)(2,1)} %bitcast.6) | data formatting | bytes 1572864

commit v6 on v5

--- a/solution.py
+++ b/solution.py
@@ -69,18 +69,6 @@
             device_id_type=pl.DeviceIdType.MESH,
         )
 
-    load_x = fetch(0, x, ext.at[pl.ds(1, rows)])
-    load_x.start()
-    taps = [fetch(1 + b, wc_hbm.at[:, b], wc.at[:, b]) for b in range(3)]
-    mats = [
-        fetch(4 + i, src, dst)
-        for i, (src, dst) in enumerate(
-            ((wq_hbm, wq), (wk_hbm, wk), (wv_hbm, wv), (wo_hbm, wo))
-        )
-    ]
-    for copy in taps + mats:
-        copy.start()
-
     barrier = pltpu.get_barrier_semaphore()
     met = 0
     for there, device in (
@@ -97,6 +85,18 @@
                 barrier, inc=1, device_id=device, device_id_type=pl.DeviceIdType.MESH
             )
 
+    load_x = fetch(0, x, ext.at[pl.ds(1, rows)])
+    load_x.start()
+    taps = [fetch(1 + b, wc_hbm.at[:, b], wc.at[:, b]) for b in range(3)]
+    mats = [
+        fetch(4 + i, src, dst)
+        for i, (src, dst) in enumerate(
+            ((wq_hbm, wq), (wk_hbm, wk), (wv_hbm, wv), (wo_hbm, wo))
+        )
+    ]
+    for copy in taps:
+        copy.start()
+
     pl.semaphore_wait(barrier, met)
 
     halo_up = send(0, x.at[0], ext.at[rows + 1], to_above)
@@ -171,6 +171,10 @@
         @pl.when(has_next)
         def _():
             moves[i].start()
+
+        if i == 0:
+            for copy in mats:
+                copy.start()
 
     mean = head_mean(chans)
 

time: 33.3 us -> 33.3 us (level)
  no operation moved by 1% of the time
where the time goes in v6:
time: 33.3 us; the launch traced here: 33.1 us
  Pallas kernels  31 us (93%)
  local copies, waits for them, and re-layouts  2.1 us (6%)
    pallas_call x1, Pallas kernels, shards(): pl.pallas_call(kernel, out_shape=jax.ShapeDtypeStruct((rows, width, chans...  31 us
    unnamed x1, local copies, waits for them, and re-layouts  2.1 us

profile of v6, /device:TPU:26, one launch (start us, length us, event | category | flops | bytes accessed | tf_op | source)
XLA Modules:
  0.0 33.1 jit_solution(4351823629947501260)
XLA Ops:
  0.0 31.0 %shard_map.109 = bf16[6,128,512]{2,1,0:T(8,128)(2,1)} custom-call(s32[1,4,6]{2,1,0:T(4,128)} %bitcast.8, s32[1,6]{1,0:T(1,128)} %valid.1, bf16[6,128,512]{2,1,0:T(8,128)(2,1)} %bitcast.7, bf16[3,3,512,512]{3,2,1,0:T(8,128)(2,1)} %wc_hbm.1, bf16[512,512]{1,0:T(8,128)(2,1)} %wq_hbm.1, bf16[512,512]{1,0:T(8,128)(2,1)} %wk_hbm.1, bf16[512,512]{1,0:T(8,128)(2,1)} %wv_hbm.1, ...), custom_call_target="tpu_custom_call" | custom-call | tf_op jit(solution)/shard_map/pallas_call | solution.py:320
  31.0 2.1 %copy.13 = bf16[1,6,128,512]{3,2,1,0:T(8,128)(2,1)} copy(bf16[1,6,128,512]{3,2,1,0:T(8,128)(2,1)} %bitcast.6) | data formatting | bytes 1572864
